TPU v7x, 32 devices: a whole 2x2x4 slice. The times are simulated.
32 devices in a mesh: groups: 2 (over y), slab: 4 (over z), coil: 2 (over x), pencil: 2 (over core).
Axes of the slice: x: 2, y: 2, z: 4, core: 2. Of those that a mesh axis runs over, the one named last changes fastest.
Arguments:
- estimate: float32 [2, 256, 128, 128], P(None, ('groups', 'slab', 'pencil'), 'coil'), parts along dimension 1, may hold values from -6 to 6
- coil_sens: bfloat16 [2, 8, 256, 128, 128], P(None, 'coil', ('groups', 'slab', 'pencil')), parts along dimension 2, may hold values from -3 to 3
- measured: bfloat16 [2, 8, 128, 256, 128], P(None, 'coil', None, ('groups', 'slab', 'pencil')), parts along dimension 3, may hold values from -4.1875 to 4.1875
- sampling: int32 [128, 256], P(None, ('groups', 'slab', 'pencil')), parts along dimension 1, may hold values 0 or 1
- step_size: float32 [1], replicated, may hold values from 0.2 to 2
- conv_in: bfloat16 [32, 2, 3, 3, 3], replicated, may hold values from -0.875 to 0.875
- bias_in: float32 [32], replicated, may hold values from -3 to 3
- conv_out: bfloat16 [2, 32, 3, 3, 3], replicated, may hold values from -0.21875 to 0.21875
Outputs:
- refined: float32 [2, 256, 128, 128], P(None, ('groups', 'slab', 'pencil'), 'coil'), parts along dimension 1
There are 2 independent parts, one for each index of `groups`. A program takes and returns all parts, laid end to end along the dimension named above; an argument that names none is the same for every part. Nothing has to cross between parts.
All inputs are finite; a program needn't handle non-finite values. No bound on the sum of `sampling` on one device may be relied on, other than what follows from the above.
Results may differ from a plain program's by a relative error of at most 0.0014.
Values may be sent and summed in bfloat16 or wider, within the bound.
No kernel may reach another device: no remote copies, remote signals or barrier semaphores. Data moves between devices by JAX's collectives and lax.ppermute only.
A program may use at most 192 MiB of HBM per device.

v0:
```python
import jax
import jax.numpy as jnp
from jax import lax
from jax.sharding import PartitionSpec as P

NY = 128
NZ = 128


PRECISE = lax.Precision.HIGHEST
LETTERS = "abcdefghij"


def extended(x, sides, width):
    for axis, dim in sides:
        size, length = (lax.axis_size(axis), x.shape[dim])
        up = [(i, (i + 1) % size) for i in range(size - 1)]
        down = [(j, i) for i, j in up]
        last = lax.slice_in_dim(x, length - width, length, axis=dim)
        initial = lax.slice_in_dim(x, 0, width, axis=dim)
        before = lax.ppermute(last, axis, up)
        after = lax.ppermute(initial, axis, down)
        x = jnp.concatenate([before, x, after], axis=dim)
    return x


def dft_table(length):
    indices = jnp.arange(length, dtype=jnp.int32)
    phases = indices[:, None] * indices[None, :] % length
    angles = phases.astype(jnp.float32) * (2.0 * jnp.pi / length)
    factor = 1.0 / jnp.sqrt(jnp.float32(length))
    return jnp.stack([jnp.cos(angles) * factor, jnp.sin(angles) * factor])


def transform(values, axis_pos, inverse):
    tables = dft_table(values.shape[axis_pos])
    rank_count = values.ndim
    source = LETTERS[:rank_count]
    target = source[:axis_pos] + "z" + source[axis_pos + 1 :]
    products_all = jnp.einsum(
        "tz" + source[axis_pos] + "," + source + "->t" + target, tables, values, precision=PRECISE
    )
    cos_real, cos_imag = (products_all[0, 0], products_all[0, 1])
    sin_real, sin_imag = (products_all[1, 0], products_all[1, 1])
    if inverse:
        return jnp.stack([cos_real - sin_imag, cos_imag + sin_real])
    return jnp.stack([cos_real + sin_imag, cos_imag - sin_real])


def complex_product(operand, partner, conjugate):
    if conjugate:
        real_part = operand[0] * partner[0] + operand[1] * partner[1]
        imag_part = operand[0] * partner[1] - operand[1] * partner[0]
    else:
        real_part = operand[0] * partner[0] - operand[1] * partner[1]
        imag_part = operand[0] * partner[1] + operand[1] * partner[0]
    return jnp.stack([real_part, imag_part])


def regularizer(estimate, conv_in, bias_in, conv_out):
    hidden_count = conv_in.shape[0]
    z_local, y_local, x_count = (estimate.shape[1], estimate.shape[2], estimate.shape[3])
    plane_input = estimate.astype(jnp.bfloat16)
    rim_depth = 2
    framed = extended(plane_input, ((("slab", "pencil"), 1), ("coil", 2)), rim_depth)
    framed = jnp.pad(framed, ((0, 0), (0, 0), (0, 0), (1, 1)))
    z_out = z_local + 2 * rim_depth - 2
    y_out = y_local + 2 * rim_depth - 2
    columns = jnp.stack(
        [
            framed[
                :, shift_z : shift_z + z_out, shift_y : shift_y + y_out, shift_x : shift_x + x_count
            ]
            for shift_z in range(3)
            for shift_y in range(3)
            for shift_x in range(3)
        ],
        axis=1,
    )
    columns = columns.reshape(2 * 27, z_out * y_out * x_count)
    kernel_in = conv_in.reshape(hidden_count, 2 * 27)
    hidden = jnp.dot(kernel_in, columns, preferred_element_type=jnp.float32) + bias_in[:, None]
    hidden = jnp.where(hidden > 0, hidden, 0.2 * hidden).reshape(
        hidden_count, z_out, y_out, x_count
    )
    z_global = lax.axis_index(("slab", "pencil")) * z_local - 1 + lax.iota(jnp.int32, z_out)
    y_global = lax.axis_index("coil") * y_local - 1 + lax.iota(jnp.int32, y_out)
    inside = ((z_global >= 0) & (z_global < NZ))[:, None] & ((y_global >= 0) & (y_global < NY))[
        None, :
    ]
    framed_hidden = jnp.where(inside[None, :, :, None], hidden, 0.0).astype(jnp.bfloat16)
    framed_hidden = jnp.pad(framed_hidden, ((0, 0), (0, 0), (0, 0), (1, 1)))
    result = jnp.zeros((2, z_local, y_local, x_count), jnp.float32)
    for shift_z in range(3):
        kernel_plane = jnp.transpose(conv_out[:, :, shift_z], (0, 2, 3, 1)).reshape(
            18, hidden_count
        )
        products = jnp.einsum(
            "qc,czyx->qzyx",
            kernel_plane,
            framed_hidden[:, shift_z : shift_z + z_local],
            preferred_element_type=jnp.float32,
        )
        products = products.reshape(2, 3, 3, z_local, y_local + 2, x_count + 2)
        for shift_y in range(3):
            for shift_x in range(3):
                result = (
                    result
                    + products[
                        :,
                        shift_y,
                        shift_x,
                        :,
                        shift_y : shift_y + y_local,
                        shift_x : shift_x + x_count,
                    ]
                )
    return result


def body(estimate, coil_sens, measured, sampling, step_size, conv_in, bias_in, conv_out):
    gathered = lax.all_gather(estimate, "coil", axis=2, tiled=True)
    coil_maps = coil_sens.astype(jnp.float32)
    coil_images = complex_product(coil_maps, gathered[:, None], False)
    spectra = transform(transform(coil_images, 4, False), 3, False)
    pencils = lax.all_to_all(spectra, ("slab", "pencil"), split_axis=3, concat_axis=2, tiled=True)
    spectra_full = transform(pencils, 2, False)
    weights = sampling.astype(jnp.float32)[None, None, :, :, None]
    misfit = weights * (spectra_full - measured.astype(jnp.float32))
    misfit_back = transform(misfit, 2, True)
    slab_view = lax.all_to_all(
        misfit_back, ("slab", "pencil"), split_axis=2, concat_axis=3, tiled=True
    )
    coil_back = transform(transform(slab_view, 3, True), 4, True)
    partial_terms = jnp.sum(complex_product(coil_maps, coil_back, True), axis=1)
    gradient = lax.psum_scatter(partial_terms, "coil", scatter_dimension=2, tiled=True)
    regular = regularizer(estimate, conv_in, bias_in, conv_out)
    return estimate - step_size[0] * gradient - regular


def solution(mesh):
    in_specs = (
        P(None, ("groups", "slab", "pencil"), "coil", None),
        P(None, "coil", ("groups", "slab", "pencil"), None, None),
        P(None, "coil", None, ("groups", "slab", "pencil"), None),
        P(None, ("groups", "slab", "pencil")),
        P(),
        P(),
        P(),
        P(),
    )
    out_specs = P(None, ("groups", "slab", "pencil"), "coil", None)
    return jax.shard_map(body, mesh=mesh, in_specs=in_specs, out_specs=out_specs, check_vma=False)
```

profile of v0, /device:TPU:15, one launch (start us, length us, event | category | flops | bytes accessed | tf_op | source)
XLA Modules:
  0.0 826.0 jit_solution(12326889238807529269)
XLA Ops:
  6.5 0.7 all-gather.2.cloned.1.call-update
  7.3 6.6 convert_element_type.40
  14.1 27.9 %all-gather.2.cloned.1.call-done = f32[2,16,128,128]{3,2,1,0:T(8,128)} async-done(((f32[2,16,64,128]{3,2,1,0:T(8,128)}), f32[2,16,128,128]{3,2,1,0:T(8,128)}) %all-gather.2.cloned.1.call-update) | async-done | bytes 2097168 | tf_op jit(solution)/shard_map/all_gather | solution.py:122
  42.0 1.8 slice_bitcast_fusion.21
  43.8 5.4 multiply_subtract_fusion.1
  49.2 13.4 %fusion.27 = f32[2,2,4,16,128,128]{5,4,0,3,2,1:T(8,128)S(1)} fusion(f32[1,4,16,128,128]{4,3,2,1,0:T(8,128)S(1)} %get-tuple-element.8, f32[1,4,16,128,128]{4,3,2,1,0:T(8,128)S(1)} %get-tuple-element.7, f32[1,128,128]{2,1,0:T(8,128)S(1)} %get-tuple-element.20, f32[1,128,128]{2,1,0:T(8,128)S(1)} %get-tuple-element.21), kind=kOutput, calls=%fused_computation.35 | convolution fusion | flops 6444580864 | bytes 25296896 | tf_op jit(solution)/shard_map/tze,abcde->tabcdz/dot_general | solution.py:40
  62.6 1.1 fusion.42
  63.7 1.1 fusion.44
  64.8 13.6 %fusion.26 = f32[2,2,4,16,128,128]{4,5,0,3,2,1:T(8,128)S(1)} fusion(f32[1,4,16,128,128]{4,3,2,1,0:T(8,128)S(1)} %fusion.42, f32[1,4,16,128,128]{4,3,2,1,0:T(8,128)S(1)} %fusion.44, f32[1,128,128]{2,1,0:T(8,128)S(1)} %get-tuple-element.20, f32[1,128,128]{2,1,0:T(8,128)S(1)} %get-tuple-element.21), kind=kOutput, calls=%fused_computation.34 | convolution fusion | flops 6444580864 | bytes 25296896 | tf_op jit(solution)/shard_map/tzd,abcde->tabcze/dot_general | solution.py:40
  78.4 1.1 fusion.39
  79.5 1.1 fusion.41
  80.6 4.3 pad_maximum_fusion
  84.9 10.3 %copy.102 = f32[2,4,16,128,128]{4,2,1,0,3:T(8,128)} copy(f32[2,4,16,128,128]{3,4,2,1,0:T(8,128)} %pad_maximum_fusion) | data formatting | bytes 16777216 | tf_op jit(solution)/shard_map/stack | solution.py:47
  95.2 5.9 all-to-all-start
  101.2 8.0 copy.108
  109.2 172.3 %all-to-all-done = f32[2,4,16,128,128]{4,2,1,0,3:T(8,128)} async-done(((f32[2,4,16,128,128]{4,2,1,0,3:T(8,128)}), f32[2,4,16,128,128]{4,2,1,0,3:T(8,128)}, u32[]{:S(2)}, u32[]{:S(2)}) %all-to-all-start) | async-done | bytes 8388640 | tf_op jit(solution)/shard_map/all_to_all | solution.py:126
  281.5 8.2 copy.104
  289.8 13.5 %fusion.22 = f32[2,2,4,128,16,128]{3,5,0,4,2,1:T(8,128)S(1)} fusion(f32[2,4,128,16,128,1]{4,3,2,1,0,5:T(8,128)S(1)} %bitcast.391, f32[1,128,128]{2,1,0:T(8,128)S(1)} %get-tuple-element.20, f32[1,128,128]{2,1,0:T(8,128)S(1)} %get-tuple-element.21), kind=kOutput, calls=%fused_computation.32 | convolution fusion | flops 6442483712 | bytes 25296896 | tf_op jit(solution)/shard_map/tzc,abcde->tabzde/dot_general | solution.py:40
  303.3 0.8 fusion.36
  304.0 3.0 fusion.38
  307.1 16.7 %fusion.19 = f32[2,2,4,128,16,128]{3,5,0,4,2,1:T(8,128)S(1)} fusion(f32[1,4,128,16,128]{2,4,3,1,0:T(8,128)S(1)} %fusion.36, f32[1,4,128,16,128]{2,4,3,1,0:T(8,128)} %fusion.38, bf16[2,4,128,16,128]{2,4,3,1,0:T(8,128)(2,1)} %copy.108, f32[128,16]{0,1:T(8,128)S(1)} %convert_element_type.41, f32[1,128,128]{2,1,0:T(8,128)S(1)} %get-tuple-element.20, ...), kind=kOutput, calls=%fused_computation.31 | convolution fusion | flops 6450872320 | bytes 29499392 | tf_op jit(solution)/shard_map/tzc,abcde->tabzde/dot_general | solution.py:40
  323.8 1.1 fusion.33
  324.9 2.7 fusion.35
  327.6 6.3 pad_maximum_fusion.1
  333.9 10.3 %copy.111 = f32[2,4,128,16,128]{4,3,1,0,2:T(8,128)} copy(f32[2,4,128,16,128]{2,4,3,1,0:T(8,128)} %pad_maximum_fusion.1) | data formatting | bytes 16777216 | tf_op jit(solution)/shard_map/stack | solution.py:46
  344.3 8.6 %all-to-all-start.1 = ((f32[2,4,128,16,128]{4,3,1,0,2:T(8,128)}), f32[2,4,128,16,128]{4,3,1,0,2:T(8,128)}, u32[]{:S(2)}, u32[]{:S(2)}) async-start(f32[2,4,128,16,128]{4,3,1,0,2:T(8,128)} %copy.111), calls=%async_computation.1 | async-start | bytes 16777216 | tf_op jit(solution)/shard_map/all_to_all | solution.py:131
  353.0 3.4 collective-permute-start
  356.4 1.9 collective-permute-start.1
  358.4 175.5 %collective-permute-done = bf16[2,2,64,128]{3,2,1,0:T(8,128)(2,1)S(1)} collective-permute-done((bf16[2,2,64,128]{3,2,1,0:T(8,128)(2,1)S(1)}, bf16[2,2,64,128]{3,2,1,0:T(8,128)(2,1)S(1)}, u32[]{:S(2)}, u32[]{:S(2)}) %collective-permute-start) | collective-permute-done | bytes 65568 | tf_op jit(solution)/shard_map/ppermute | solution.py:21
  533.9 1.8 collective-permute-done.1
  535.8 1.3 collective-permute-start.2
  537.1 4.2 collective-permute-start.3
  541.3 2.1 copy.121
  543.5 0.6 reshape.406
  546.3 0.4 fusion.63
  547.0 0.4 fusion.65
  547.4 0.4 fusion.67
  548.0 0.4 fusion.69
  550.0 0.4 fusion.77
  550.4 0.4 fusion.79
  551.0 0.4 fusion.81
  552.3 0.4 fusion.87
  554.4 6.5 copy.122
  560.9 17.6 %reshape.376 = bf16[54,152064]{1,0:T(8,128)(2,1)} reshape(bf16[2,27,18,66,128]{4,3,2,1,0:T(8,128)(2,1)} %copy.122) | data formatting | bytes 32845824 | tf_op jit(solution)/shard_map/reshape | solution.py:80
  578.5 9.8 %compare_select_fusion = bf16[32,152064]{1,0:T(8,128)(2,1)} fusion(bf16[54,152064]{1,0:T(8,128)(2,1)} %reshape.376, bf16[32,54]{0,1:T(8,128)(2,1)S(1)} %reshape.377, f32[32]{0:T(128)S(1)} %copy-done.6), kind=kOutput, calls=%fused_computation.2 | convolution fusion | flops 544997376 | bytes 26158592 | tf_op jit(solution)/shard_map/dot_general | solution.py:82
  588.2 10.2 %reshape.378 = bf16[32,18,66,128]{3,2,1,0:T(8,128)(2,1)} reshape(bf16[32,152064]{1,0:T(8,128)(2,1)} %compare_select_fusion) | data formatting | bytes 19464192 | tf_op jit(solution)/shard_map/reshape | solution.py:83
  598.5 22.3 %copy.124 = bf16[32,18,66,128]{2,0,3,1:T(8,128)(2,1)} copy(bf16[32,18,66,128]{3,2,1,0:T(8,128)(2,1)} %reshape.378) | data formatting | bytes 19464192 | tf_op jit(solution)/shard_map/reshape | solution.py:83
  620.8 4.7 copy.113
  625.4 13.7 %convolution_bitcast_fusion.3 = f32[2,2,4,16,128,128]{4,5,0,3,2,1:T(8,128)S(1)} fusion(f32[2,4,16,128,128,1]{4,3,5,2,1,0:T(8,128)S(1)} %bitcast.392, f32[1,128,128]{2,1,0:T(8,128)S(1)} %get-tuple-element.20, f32[1,128,128]{2,1,0:T(8,128)S(1)} %get-tuple-element.21), kind=kOutput, calls=%fused_computation.36 | convolution fusion | flops 6442483712 | bytes 25296896 | tf_op jit(solution)/shard_map/tzd,abcde->tabcze/dot_general | solution.py:40
  639.1 1.1 fusion.30
  640.2 3.1 fusion.32
  643.2 17.3 %fusion.25 = f32[2,2,4,16,128,128]{5,4,3,2,1,0:T(8,128)} fusion(f32[1,4,16,128,128]{3,4,2,1,0:T(8,128)S(1)} %fusion.30, f32[1,4,16,128,128]{3,4,2,1,0:T(8,128)} %fusion.32, f32[1,128,128]{2,1,0:T(8,128)S(1)} %get-tuple-element.20, f32[1,128,128]{2,1,0:T(8,128)S(1)} %get-tuple-element.21), kind=kOutput, calls=%fused_computation.33 | convolution fusion | flops 6444580864 | bytes 25296896 | tf_op jit(solution)/shard_map/tze,abcde->tabcdz/dot_general | solution.py:40
  660.5 7.7 multiply_add_fusion
  668.2 1.0 maximum_reduce_fusion
  669.2 2.6 copy.119
  671.8 17.8 %convolution_bitcast_fusion.2 = f32[18,16,66,130]{2,0,3,1:T(8,128)} fusion(bf16[18,32,1,1]{1,0,2,3:T(8,128)(2,1)S(1)} %reshape.404, bf16[32,18,66,128]{2,0,3,1:T(8,128)(2,1)} %copy.124, pred[18,66]{1,0:T(8,128)(4,1)S(1)} %broadcast_and_fusion), kind=kOutput, calls=%fused_computation.6 | convolution fusion | flops 160579584 | bytes 19618596 | tf_op jit(solution)/shard_map/qc,czyx->qzyx/dot_general | solution.py:98
  689.5 20.8 %copy.126 = f32[18,16,66,130]{2,1,3,0:T(8,128)} copy(f32[18,16,66,130]{2,0,3,1:T(8,128)} %convolution_bitcast_fusion.2) | data formatting | bytes 19768320 | tf_op jit(solution)/shard_map/qc,czyx->qzyx/dot_general | solution.py:98
  710.3 17.7 %convolution_bitcast_fusion.1 = f32[18,16,66,130]{2,0,3,1:T(8,128)} fusion(bf16[18,32,1,1]{1,0,2,3:T(8,128)(2,1)S(1)} %reshape.405, bf16[32,18,66,128]{2,0,3,1:T(8,128)(2,1)} %copy.124, pred[18,66]{1,0:T(8,128)(4,1)S(1)} %broadcast_and_fusion), kind=kOutput, calls=%fused_computation.5 | convolution fusion | flops 160579584 | bytes 19618596 | tf_op jit(solution)/shard_map/qc,czyx->qzyx/dot_general | solution.py:98
  728.0 20.9 %copy.128 = f32[18,16,66,130]{2,1,3,0:T(8,128)} copy(f32[18,16,66,130]{2,0,3,1:T(8,128)} %convolution_bitcast_fusion.1) | data formatting | bytes 19768320 | tf_op jit(solution)/shard_map/qc,czyx->qzyx/dot_general | solution.py:98
  748.9 17.7 %convolution_bitcast_fusion = f32[18,16,66,130]{2,0,3,1:T(8,128)} fusion(bf16[18,32,1,1]{1,0,2,3:T(8,128)(2,1)S(1)} %copy-done.2, bf16[32,18,66,128]{2,0,3,1:T(8,128)(2,1)} %copy.124, pred[18,66]{1,0:T(8,128)(4,1)S(1)} %broadcast_and_fusion), kind=kOutput, calls=%fused_computation.4 | convolution fusion | flops 160579584 | bytes 19618596 | tf_op jit(solution)/shard_map/qc,czyx->qzyx/dot_general | solution.py:98
  766.6 20.7 %copy.131 = f32[18,16,66,130]{2,1,3,0:T(8,128)} copy(f32[18,16,66,130]{2,0,3,1:T(8,128)} %convolution_bitcast_fusion) | data formatting | bytes 19768320 | tf_op jit(solution)/shard_map/qc,czyx->qzyx/dot_general | solution.py:98
  787.2 3.8 copy.120
  791.1 24.3 %fusion.47 = f32[2,16,64,128]{2,1,3,0:T(8,128)} fusion(f32[2,3,3,16,66,130]{4,3,5,2,1,0:T(8,128)} %bitcast.390, f32[2,3,3,16,66,130]{4,3,5,2,1,0:T(8,128)} %bitcast.389, f32[2,3,3,16,66,130]{4,3,5,2,1,0:T(8,128)} %bitcast.388, f32[2,16,64,128]{2,1,3,0:T(8,128)S(1)} %copy-done.1, f32[2,16,64,128]{2,1,3,0:T(8,128)} %copy.120, f32[]{:T(128)} %bitcast.387), kind=kLoop, calls=%fused_computation.96 | loop fusion | flops 7602176 | bytes 31457284 | tf_op jit(solution)/shard_map/sub | solution.py:138
  815.4 3.3 copy.141
  (63 shorter events, 6.6 us)
Async XLA Ops:
  6.5 35.5 %all-gather.2.cloned.1.call-start = ((), (), s32[]{:S(2)}) async-start(), calls=%async_computation.3 | async-start | bytes 3145728 | tf_op jit(solution)/shard_map/all_gather | solution.py:122
  95.2 186.3 %all-to-all-start = ((f32[2,4,16,128,128]{4,2,1,0,3:T(8,128)}), f32[2,4,16,128,128]{4,2,1,0,3:T(8,128)}, u32[]{:S(2)}, u32[]{:S(2)}) async-start(f32[2,4,16,128,128]{4,2,1,0,3:T(8,128)} %copy.102), calls=%async_computation | async-start | bytes 16777216 | tf_op jit(solution)/shard_map/all_to_all | solution.py:126
  101.2 8.0 copy-start.5
  344.3 8.6 %copy-start = (f32[2,16,64,128]{3,2,1,0:T(8,128)S(1)}, f32[2,16,64,128]{3,2,1,0:T(8,128)}, u32[]{:S(2)}) copy-start(f32[2,16,64,128]{3,2,1,0:T(8,128)} %param.8) | copy-start | bytes 3145732
  344.3 14.1 %copy-start.3 = (bf16[2,32,3,3,3]{1,0,4,3,2:T(2,128)(2,1)S(1)}, bf16[2,32,3,3,3]{1,0,4,3,2:T(2,128)(2,1)}, u32[]{:S(2)}) copy-start(bf16[2,32,3,3,3]{1,0,4,3,2:T(2,128)(2,1)} %param.15) | copy-start | bytes 10372
  344.3 276.5 %all-to-all-start.1 = ((f32[2,4,128,16,128]{4,3,1,0,2:T(8,128)}), f32[2,4,128,16,128]{4,3,1,0,2:T(8,128)}, u32[]{:S(2)}, u32[]{:S(2)}) async-start(f32[2,4,128,16,128]{4,3,1,0,2:T(8,128)} %copy.111), calls=%async_computation.1 | async-start | bytes 16777216 | tf_op jit(solution)/shard_map/all_to_all | solution.py:131
  352.9 190.5 %copy-start.4 = (bf16[32,2,3,3,3]{0,1,4,3,2:T(2,128)(2,1)S(1)}, bf16[32,2,3,3,3]{0,1,4,3,2:T(2,128)(2,1)}, u32[]{:S(2)}) copy-start(bf16[32,2,3,3,3]{0,1,4,3,2:T(2,128)(2,1)} %param.13) | copy-start | bytes 10372
  352.9 434.3 %reduce-scatter.2.cloned.1.call-start = ((), (), s32[]{:S(2)}) async-start(), calls=%async_computation.4 | async-start | bytes 3145728 | tf_op jit(solution)/shard_map/reduce_scatter | solution.py:136
  353.0 180.9 %collective-permute-start = (bf16[2,2,64,128]{3,2,1,0:T(8,128)(2,1)S(1)}, bf16[2,2,64,128]{3,2,1,0:T(8,128)(2,1)S(1)}, u32[]{:S(2)}, u32[]{:S(2)}) collective-permute-start(bf16[2,2,64,128]{3,2,1,0:T(8,128)(2,1)S(1)} %get-tuple-element.15), channel_id=1, source_target_pairs={{0,1},{1,4},{4,5},{5,8},{8,9},{9,12},{12,13},{2,3},{3,6},{6,7},{7,... | collective-permute-start | bytes 196616 | tf_op jit(solution)/shard_map/ppermute | solution.py:21
  356.4 179.3 %collective-permute-start.1 = (bf16[2,2,64,128]{3,2,1,0:T(8,128)(2,1)S(1)}, bf16[2,2,64,128]{3,2,1,0:T(8,128)(2,1)S(1)}, u32[]{:S(2)}, u32[]{:S(2)}) collective-permute-start(bf16[2,2,64,128]{3,2,1,0:T(8,128)(2,1)S(1)} %get-tuple-element.16), channel_id=1, source_target_pairs={{1,0},{4,1},{5,4},{8,5},{9,8},{12,9},{13,12},{3,2},{6,3},{7,6},{10... | collective-permute-start | bytes 196616 | tf_op jit(solution)/shard_map/ppermute | solution.py:22
  535.8 9.0 %collective-permute-start.2 = (bf16[2,20,2,128]{3,2,1,0:T(2,128)(2,1)S(1)}, bf16[2,20,2,128]{3,2,1,0:T(2,128)(2,1)S(1)}, u32[]{:S(2)}, u32[]{:S(2)}) collective-permute-start(bf16[2,20,2,128]{3,2,1,0:T(2,128)(2,1)S(1)} %get-tuple-element.13), channel_id=1, source_target_pairs={{0,2},{1,3},{4,6},{5,7},{8,10},{9,11},{12,14},{13,15},{16,18},{17,... | collective-permute-start | bytes 61448 | tf_op jit(solution)/shard_map/ppermute | solution.py:21
  537.1 7.7 collective-permute-start.3
  560.9 17.6 %copy-start.6 = (f32[32]{0:T(128)S(1)}, f32[32]{0:T(128)}, u32[]{:S(2)}) copy-start(f32[32]{0:T(128)} %param.14) | copy-start | bytes 388
  640.2 20.3 %slice-start = ((s8[8388608]{0:T(1024)(128)(4,1)}), s8[4194304]{0:T(1024)(128)(4,1)S(1)}, s32[]{:S(2)}) async-start(s8[8388608]{0:T(1024)(128)(4,1)} %bitcast.393), calls=%async_computation.5 | async-start | bytes 8388608
  643.2 17.3 %slice-start.1 = ((s8[8388608]{0:T(1024)(128)(4,1)}), s8[4194304]{0:T(1024)(128)(4,1)S(1)}, s32[]{:S(2)}) async-start(s8[8388608]{0:T(1024)(128)(4,1)} %bitcast.393), calls=%async_computation.6 | async-start | bytes 8388608
  728.0 20.9 %copy-start.2 = (bf16[18,32,1,1]{1,0,2,3:T(8,128)(2,1)S(1)}, bf16[18,32,1,1]{1,0,2,3:T(8,128)(2,1)}, u32[]{:S(2)}) copy-start(bf16[18,32,1,1]{1,0,2,3:T(8,128)(2,1)} %reshape.406) | copy-start | bytes 3460
  787.2 3.8 copy-start.1
Sparse Core Ops, SparseCore 0:
  8.9 33.0 all-gather.1
  671.9 30.2 reduce-scatter.1
where the time goes:
time: 837 us; the launch traced here: 826 us
  waiting for transfers between devices  378 us (45%)
  local copies, waits for them, and re-layouts  184 us (22%)
  matrix products  151 us (18%)
  other arithmetic  72.9 us (9%)
  starting transfers between devices  25.3 us (3%)
  between operations  14.9 us (2%)
    ppermute x2, waiting for transfers between devices, extended(): before = lax.ppermute(last, axis, up)  176 us
    all_to_all x1, waiting for transfers between devices, body(): lax.all_to_all(spectra, ('slab', 'pencil'), split_axis=3, concat_axis=2,...  172 us
    dot_general x6, matrix products, transform(): jnp.einsum('tz' + source[axis_pos] + ',' + source + '->t' + target, table...  88.2 us
    dot_general x3, local copies, waits for them, and re-layouts, regularizer(): jnp.einsum('qc,czyx->qzyx', kernel_plane, framed_hidden[:, shift_z:shift_...  62.4 us
    dot_general x3, matrix products, regularizer(): jnp.einsum('qc,czyx->qzyx', kernel_plane, framed_hidden[:, shift_z:shift_...  53.1 us
    reshape x2, local copies, waits for them, and re-layouts, regularizer(): jnp.where(hidden > 0, hidden, 0.2 * hidden)  32.5 us
    all_gather x1, waiting for transfers between devices, body(): gathered = lax.all_gather(estimate, 'coil', axis=2, tiled=True)  27.9 us
    sub x1, other arithmetic, body(): return estimate - step_size[0] * gradient - regular  24.3 us
  transfers between devices with their start and end apart: 8, of which 4 were waited for; matrix products, arithmetic and copies ran while one was open for 25% of the time, Pallas kernels for 0%

commit v1 on v0

--- a/solution.py
+++ b/solution.py
@@ -1,14 +1,338 @@
+import functools
+import math
+
 import jax
 import jax.numpy as jnp
+import numpy as np
 from jax import lax
+from jax.experimental import pallas as pl
+from jax.experimental.pallas import tpu as pltpu
 from jax.sharding import PartitionSpec as P
 
-NY = 128
-NZ = 128
-
-
-PRECISE = lax.Precision.HIGHEST
-LETTERS = "abcdefghij"
+LINE = ("slab", "pencil")
+HALF = jnp.float16
+F32 = jnp.float32
+BF16 = jnp.bfloat16
+SCALE = 1.0 / 16.0
+
+
+def line_dft(n):
+    k = np.arange(n)
+    angles = 2.0 * np.pi * (k[:, None] * k[None, :] % n) / n
+    c, s = np.cos(angles) / math.sqrt(n), np.sin(angles) / math.sqrt(n)
+    return np.block([[c, s], [-s, c]])
+
+
+def split(table):
+    high = table.astype(BF16)
+    low = (table - high.astype(np.float64)).astype(BF16)
+    return np.stack([high, low])
+
+
+def dot(a, b):
+    return jnp.dot(a, b, preferred_element_type=F32)
+
+
+def dot3(table, data):
+    high = data.astype(BF16)
+    low = (data - high.astype(F32)).astype(BF16)
+    return dot(table[0], high) + dot(table[1], high) + dot(table[0], low)
+
+
+def forward_y_kernel(place_ref, own_ref, other_ref, sens_ref, table_ref, out_ref):
+    first = place_ref[0] == 0
+    zl = own_ref.shape[1]
+    blocks = out_ref.shape[0]
+    kyl = out_ref.shape[3] // zl
+    n = 2 * own_ref.shape[2]
+    table = (table_ref[0], table_ref[1])
+
+    def image(z):
+        parts = []
+        for ri in range(2):
+            own, other = own_ref[ri, z], other_ref[ri, z].astype(F32)
+            top = jnp.where(first, own, other)
+            bottom = jnp.where(first, other, own)
+            parts.append(jnp.concatenate([top, bottom], axis=0))
+        sr, si = sens_ref[0, 0, z].astype(F32), sens_ref[1, 0, z].astype(F32)
+        re = sr * parts[0] - si * parts[1]
+        im = sr * parts[1] + si * parts[0]
+        return jnp.concatenate([re, im], axis=0)
+
+    def step(p, carry):
+        data = jnp.concatenate([image(2 * p), image(2 * p + 1)], axis=1)
+        result = dot3(table, data)
+        x = result.shape[1] // 2
+        for half in range(2):
+            for d in range(blocks):
+                for ro in range(2):
+                    rows = result[ro * n + d * kyl : ro * n + (d + 1) * kyl, half * x : (half + 1) * x]
+                    out_ref[d, 0, ro, pl.ds(2 * p + half, kyl, stride=zl), :] = rows
+        return carry
+
+    lax.fori_loop(0, zl // 2, step, 0)
+
+
+def forward_y(place, own, other, sens, table, blocks):
+    _, nc, zl, n, x = sens.shape
+    kyl = n // blocks
+    return pl.pallas_call(
+        forward_y_kernel,
+        grid=(nc,),
+        in_specs=[
+            pl.BlockSpec(memory_space=pltpu.SMEM),
+            pl.BlockSpec(own.shape, lambda c: (0, 0, 0, 0)),
+            pl.BlockSpec(other.shape, lambda c: (0, 0, 0, 0)),
+            pl.BlockSpec((2, 1, zl, n, x), lambda c: (0, c, 0, 0, 0)),
+            pl.BlockSpec(table.shape, lambda c: (0, 0, 0)),
+        ],
+        out_specs=pl.BlockSpec((blocks, 1, 2, kyl * zl, x), lambda c: (0, c, 0, 0, 0)),
+        out_shape=jax.ShapeDtypeStruct((blocks, nc, 2, kyl * zl, x), F32),
+        cost_estimate=pl.CostEstimate(
+            flops=2 * 3 * 2 * n * 2 * n * nc * zl * x, bytes_accessed=14 * sens.size // 2, transcendentals=0
+        ),
+        name="forward_y",
+    )(place, own, other, sens, table)
+
+
+def middle_kernel(in_ref, circ_ref, meas_ref, out_ref):
+    blocks, nc = in_ref.shape[0], in_ref.shape[1]
+    kys = circ_ref.shape[1]
+    zl = in_ref.shape[3] // kys
+    x = in_ref.shape[4]
+    n = blocks * zl
+    for k in range(kys):
+        columns = []
+        for c in range(nc):
+            rows = [in_ref[s, c, ri, k * zl : (k + 1) * zl, :] for ri in range(2) for s in range(blocks)]
+            columns.append(jnp.concatenate(rows, axis=0))
+        data = jnp.concatenate(columns, axis=1)
+        result = dot3((circ_ref[0, k], circ_ref[1, k]), data) - meas_ref[k]
+        for c in range(nc):
+            for ri in range(2):
+                for d in range(blocks):
+                    out_ref[d, c, ri, k * zl : (k + 1) * zl, :] = result[
+                        ri * n + d * zl : ri * n + (d + 1) * zl, c * x : (c + 1) * x
+                    ]
+
+
+def middle(data, circ, meas):
+    blocks, nc, _, rows, x = data.shape
+    kyl, n2 = circ.shape[1], circ.shape[2]
+    zl = rows // kyl
+    kb = 2
+    block = (blocks, nc, 2, kb * zl, x)
+    return pl.pallas_call(
+        middle_kernel,
+        grid=(kyl // kb,),
+        in_specs=[
+            pl.BlockSpec(block, lambda k: (0, 0, 0, k, 0)),
+            pl.BlockSpec((2, kb, n2, n2), lambda k: (0, k, 0, 0)),
+            pl.BlockSpec((kb, n2, nc * x), lambda k: (k, 0, 0)),
+        ],
+        out_specs=pl.BlockSpec(block, lambda k: (0, 0, 0, k, 0)),
+        out_shape=jax.ShapeDtypeStruct(data.shape, F32),
+        cost_estimate=pl.CostEstimate(
+            flops=2 * 3 * n2 * n2 * kyl * nc * x, bytes_accessed=12 * data.size, transcendentals=0
+        ),
+        name="middle_z",
+    )(data, circ, meas)
+
+
+def backward_y_kernel(in_ref, sens_ref, table_ref, out_ref):
+    blocks = in_ref.shape[0]
+    zl = out_ref.shape[1]
+    n, x = out_ref.shape[2], out_ref.shape[3]
+    kyl = n // blocks
+    table = (table_ref[0], table_ref[1])
+
+    @pl.when(pl.program_id(0) == 0)
+    def _():
+        out_ref[...] = jnp.zeros_like(out_ref)
+
+    def step(p, carry):
+        columns = []
+        for half in range(2):
+            rows = [
+                in_ref[s, 0, ri, pl.ds(2 * p + half, kyl, stride=zl), :] for ri in range(2) for s in range(blocks)
+            ]
+            columns.append(jnp.concatenate(rows, axis=0))
+        result = dot3(table, jnp.concatenate(columns, axis=1))
+        for half in range(2):
+            z = 2 * p + half
+            cr = result[:n, half * x : (half + 1) * x]
+            ci = result[n:, half * x : (half + 1) * x]
+            sr, si = sens_ref[0, 0, z].astype(F32), sens_ref[1, 0, z].astype(F32)
+            out_ref[0, z] += sr * cr + si * ci
+            out_ref[1, z] += sr * ci - si * cr
+        return carry
+
+    lax.fori_loop(0, zl // 2, step, 0)
+
+
+def backward_y(data, sens, table):
+    _, nc, zl, n, x = sens.shape
+    blocks = data.shape[0]
+    return pl.pallas_call(
+        backward_y_kernel,
+        grid=(nc,),
+        in_specs=[
+            pl.BlockSpec((blocks, 1, 2, data.shape[3], x), lambda c: (0, c, 0, 0, 0)),
+            pl.BlockSpec((2, 1, zl, n, x), lambda c: (0, c, 0, 0, 0)),
+            pl.BlockSpec(table.shape, lambda c: (0, 0, 0)),
+        ],
+        out_specs=pl.BlockSpec((2, zl, n, x), lambda c: (0, 0, 0, 0)),
+        out_shape=jax.ShapeDtypeStruct((2, zl, n, x), F32),
+        cost_estimate=pl.CostEstimate(
+            flops=2 * 3 * 2 * n * 2 * n * nc * zl * x, bytes_accessed=14 * sens.size // 2, transcendentals=0
+        ),
+        name="backward_y",
+    )(data, sens, table)
+
+
+def measured_images(measured, sampling, table_z, table_x):
+    _, nc, nz, kyl, nx = measured.shape
+    masked = jnp.where((sampling > 0)[None, None, :, :, None], measured, 0).astype(BF16)
+    tx = table_x.reshape(2, 2, nx, 2, nx)
+    form = "pfqx,pczkf->kqzcx"
+    along_x = jnp.einsum(form, tx[0], masked, preferred_element_type=F32)
+    along_x = along_x + jnp.einsum(form, tx[1], masked, preferred_element_type=F32)
+    high = lax.reduce_precision(along_x, 8, 7)
+    low = (along_x - high).astype(BF16)
+    high = high.astype(BF16)
+    stacked = jnp.stack([high, low])
+    tz = table_z.reshape(2, 2, nz, 2, nz)
+    tz = jnp.stack([tz[0], tz[0], tz[1]])
+    stacked = jnp.stack([high, low, high])
+    out = jnp.einsum("tpzqw,tkpzcx->kqwcx", tz, stacked, preferred_element_type=F32)
+    return out.reshape(kyl, 2 * nz, nc * nx)
+
+
+def circulants(sampling, table_z):
+    nz = sampling.shape[0]
+    weights = (sampling > 0).astype(BF16).T
+    weights = jnp.concatenate([weights, weights], axis=1)
+    left = jnp.concatenate([table_z[0], table_z[1], table_z[0]], axis=0)
+    right = jnp.concatenate([table_z[0], table_z[0], table_z[1]], axis=0)
+    scaled = right[None] * jnp.tile(weights, (1, 3))[:, :, None]
+    circ = jnp.einsum("kw,ykz->ywz", left, scaled, preferred_element_type=F32)
+    high = lax.reduce_precision(circ, 8, 7)
+    return jnp.stack([high.astype(BF16), (circ - high).astype(BF16)])
+
+
+def conv_kernel(edge_ref, frame_ref, w1_ref, w2_ref, bias_ref, out_ref, cols_ref, acc_ref, *, nyb, hid):
+    planes = frame_ref.shape[1]
+    x = frame_ref.shape[3]
+    rows = cols_ref.shape[0] // planes
+    lane = lax.broadcasted_iota(jnp.int32, (24, x), 1)
+    acc_ref[...] = jnp.zeros_like(acc_ref)
+
+    def gather(z, carry):
+        pieces = []
+        for c in range(2):
+            blocks = [frame_ref[c, z, yb * 16 : yb * 16 + 24, :] for yb in range(nyb)]
+            for d in range(3):
+                if d == 0:
+                    moved = [jnp.where(lane == 0, 0.0, pltpu.roll(b, 1, 1)) for b in blocks]
+                elif d == 2:
+                    moved = [jnp.where(lane == x - 1, 0.0, pltpu.roll(b, x - 1, 1)) for b in blocks]
+                else:
+                    moved = blocks
+                pieces.append(jnp.concatenate(moved, axis=1))
+        cols_ref[pl.ds(pl.multiple_of(z * rows, 16), rows), :] = jnp.concatenate(pieces, axis=0).astype(BF16)
+        return carry
+
+    lax.fori_loop(0, planes, gather, 0)
+    lane16 = lax.broadcasted_iota(jnp.int32, (32, x), 1)
+
+    def plane(z, carry):
+        cols = cols_ref[pl.ds(pl.multiple_of(z * rows, 16), 3 * rows), :]
+        hidden = dot(w1_ref[...], cols)
+        hidden = hidden + jnp.concatenate([bias_ref[...]] * nyb, axis=1)
+        hidden = jnp.where(hidden > 0, hidden, 0.2 * hidden)
+        top = hidden[:hid] * jnp.concatenate(
+            [jnp.full((hid, x), edge_ref[0], F32)] + [jnp.ones((hid, x), F32)] * (nyb - 1), axis=1
+        )
+        bottom = hidden[-hid:] * jnp.concatenate(
+            [jnp.ones((hid, x), F32)] * (nyb - 1) + [jnp.full((hid, x), edge_ref[1], F32)], axis=1
+        )
+        hidden = jnp.concatenate([top, hidden[hid:-hid], bottom], axis=0).astype(BF16)
+        products = dot(w2_ref[...], hidden)
+        z_global = edge_ref[2] + z
+        keep = jnp.where((z_global >= 0) & (z_global < edge_ref[3]), 1, 0).astype(F32)
+        for a in range(3):
+            for yb in range(nyb):
+                p = [products[(a * 3 + d) * 32 : (a * 3 + d + 1) * 32, yb * x : (yb + 1) * x] for d in range(3)]
+                total = (
+                    p[1]
+                    + jnp.where(lane16 == 0, 0.0, pltpu.roll(p[0], 1, 1))
+                    + jnp.where(lane16 == x - 1, 0.0, pltpu.roll(p[2], x - 1, 1))
+                )
+                acc_ref[z + 2 - a, :, yb * x : (yb + 1) * x] += keep * total
+        return carry
+
+    lax.fori_loop(0, planes - 2, plane, 0)
+
+    def emit(z, carry):
+        for q in range(2):
+            for yb in range(nyb):
+                out_ref[q, z, yb * 16 : (yb + 1) * 16, :] = acc_ref[z + 2, q * 16 : (q + 1) * 16, yb * x : (yb + 1) * x]
+        return carry
+
+    lax.fori_loop(0, out_ref.shape[1], emit, 0)
+
+
+def band_weights(conv_in, conv_out):
+    hid = conv_in.shape[0]
+    shift = np.arange(3)
+    w = jnp.transpose(conv_in, (3, 0, 2, 1, 4)).reshape(3, hid, 18)
+    spread = np.repeat(np.eye(18), 24, axis=1).astype(BF16)
+    wide = jnp.einsum("bok,kl->bol", w, spread, preferred_element_type=F32)
+    hit = np.arange(18)[None, :, None] + shift[:, None, None] == np.arange(24)[None, None, :]
+    hit = np.tile(hit, (1, 1, 18)).astype(np.float32)
+    w1 = jnp.sum(wide[:, None] * hit[:, :, None, :], axis=0).astype(BF16).reshape(18 * hid, 18 * 24)
+    v = jnp.transpose(conv_out, (3, 2, 4, 0, 1)).reshape(3, 18, hid)
+    spread = np.tile(np.eye(hid), (1, 18)).astype(BF16)
+    wide = jnp.einsum("bko,ol->bkl", v, spread, preferred_element_type=F32)
+    hit = np.arange(16)[None, :, None] + shift[:, None, None] == np.arange(18)[None, None, :]
+    hit = np.repeat(hit, hid, axis=2).astype(np.float32)
+    w2 = jnp.sum(wide[:, :, None] * hit[:, None], axis=0).astype(BF16).reshape(18 * 16, 18 * hid)
+    return w1, w2
+
+
+def regularizer(framed, conv_in, bias_in, conv_out, size_z):
+    hid = conv_in.shape[0]
+    _, planes, yframe, x = framed.shape
+    zl, yl = planes - 4, yframe - 4
+    nyb = yl // 16
+    w1, w2 = band_weights(conv_in, conv_out)
+    bias = jnp.broadcast_to(jnp.tile(bias_in, 18)[:, None], (18 * hid, x))
+    frame = jnp.pad(framed.astype(F32), ((0, 0), (0, 0), (0, 4), (0, 0)))
+    last = lax.axis_size("coil") - 1
+    at = lax.axis_index("coil")
+    edges = jnp.stack(
+        [
+            (at > 0).astype(jnp.int32),
+            (at < last).astype(jnp.int32),
+            (lax.axis_index(LINE) * zl - 1).astype(jnp.int32),
+            jnp.int32(size_z),
+        ]
+    )
+    vmem = pl.BlockSpec(memory_space=pltpu.VMEM)
+    return pl.pallas_call(
+        functools.partial(conv_kernel, nyb=nyb, hid=hid),
+        in_specs=[pl.BlockSpec(memory_space=pltpu.SMEM)] + [vmem] * 4,
+        out_specs=vmem,
+        out_shape=jax.ShapeDtypeStruct((2, zl, yl, x), F32),
+        scratch_shapes=[
+            pltpu.VMEM((planes * 144, nyb * x), BF16),
+            pltpu.VMEM((zl + 4, 32, nyb * x), F32),
+        ],
+        cost_estimate=pl.CostEstimate(
+            flops=2 * (zl + 2) * nyb * x * (576 * 432 + 288 * 576), bytes_accessed=4 << 20, transcendentals=0
+        ),
+        name="regularizer",
+    )(edges, frame, w1, w2, bias)
 
 
 def extended(x, sides, width):
@@ -24,6 +348,39 @@
     return x
 
 
+def fast_body(estimate, coil_sens, measured, sampling, step_size, conv_in, bias_in, conv_out):
+    _, nc, zl, ny, nx = coil_sens.shape
+    nz = measured.shape[2]
+    yl = estimate.shape[2]
+    blocks = lax.axis_size(LINE)
+    swap = [(0, 1), (1, 0)]
+    at = lax.axis_index("coil")
+    table_y = jnp.asarray(split(line_dft(ny)))
+    table_z = jnp.asarray(split(line_dft(nz)))
+    table_x = jnp.asarray(split(line_dft(nx)))
+    back_y = jnp.asarray(split(line_dft(ny).T))
+
+    other = lax.ppermute(estimate.astype(HALF), "coil", swap).astype(F32)
+    framed = extended(estimate.astype(BF16), ((LINE, 1), ("coil", 2)), 2)
+    place = jnp.reshape(at, (1,)).astype(jnp.int32)
+    sent = forward_y(place, estimate, other, coil_sens, table_y, blocks)
+    lines = lax.all_to_all(sent.astype(HALF), LINE, split_axis=0, concat_axis=0, tiled=True)
+    circ = circulants(sampling, table_z)
+    meas = measured_images(measured, sampling, table_z, table_x)
+    back = middle(lines.astype(F32), circ, meas)
+    regular = regularizer(framed, conv_in, bias_in, conv_out, nz)
+    slabs = lax.all_to_all(back.astype(HALF), LINE, split_axis=0, concat_axis=0, tiled=True)
+    partial = backward_y(slabs.astype(F32), coil_sens, back_y)
+    mine = lax.dynamic_slice_in_dim(partial, at * yl, yl, axis=2)
+    theirs = lax.dynamic_slice_in_dim(partial, (1 - at) * yl, yl, axis=2)
+    received = lax.ppermute((theirs * SCALE).astype(HALF), "coil", swap).astype(F32) * (1.0 / SCALE)
+    return estimate - step_size[0] * (mine + received) - regular
+
+
+PRECISE = lax.Precision.HIGHEST
+LETTERS = "abcdefghij"
+
+
 def dft_table(length):
     indices = jnp.arange(length, dtype=jnp.int32)
     phases = indices[:, None] * indices[None, :] % length
@@ -57,7 +414,7 @@
     return jnp.stack([real_part, imag_part])
 
 
-def regularizer(estimate, conv_in, bias_in, conv_out):
+def generic_regularizer(estimate, conv_in, bias_in, conv_out, size_z, size_y):
     hidden_count = conv_in.shape[0]
     z_local, y_local, x_count = (estimate.shape[1], estimate.shape[2], estimate.shape[3])
     plane_input = estimate.astype(jnp.bfloat16)
@@ -85,7 +442,7 @@
     )
     z_global = lax.axis_index(("slab", "pencil")) * z_local - 1 + lax.iota(jnp.int32, z_out)
     y_global = lax.axis_index("coil") * y_local - 1 + lax.iota(jnp.int32, y_out)
-    inside = ((z_global >= 0) & (z_global < NZ))[:, None] & ((y_global >= 0) & (y_global < NY))[
+    inside = ((z_global >= 0) & (z_global < size_z))[:, None] & ((y_global >= 0) & (y_global < size_y))[
         None, :
     ]
     framed_hidden = jnp.where(inside[None, :, :, None], hidden, 0.0).astype(jnp.bfloat16)
@@ -118,7 +475,7 @@
     return result
 
 
-def body(estimate, coil_sens, measured, sampling, step_size, conv_in, bias_in, conv_out):
+def generic_body(estimate, coil_sens, measured, sampling, step_size, conv_in, bias_in, conv_out):
     gathered = lax.all_gather(estimate, "coil", axis=2, tiled=True)
     coil_maps = coil_sens.astype(jnp.float32)
     coil_images = complex_product(coil_maps, gathered[:, None], False)
@@ -134,8 +491,19 @@
     coil_back = transform(transform(slab_view, 3, True), 4, True)
     partial_terms = jnp.sum(complex_product(coil_maps, coil_back, True), axis=1)
     gradient = lax.psum_scatter(partial_terms, "coil", scatter_dimension=2, tiled=True)
-    regular = regularizer(estimate, conv_in, bias_in, conv_out)
+    regular = generic_regularizer(
+        estimate, conv_in, bias_in, conv_out, measured.shape[2], coil_sens.shape[3]
+    )
     return estimate - step_size[0] * gradient - regular
+
+
+def body(*arrays):
+    estimate, coil_sens = arrays[0], arrays[1]
+    _, zl, yl, nx = estimate.shape
+    ny = coil_sens.shape[3]
+    kyl = ny // lax.axis_size(LINE)
+    fits = zl % 16 == 0 and kyl % 16 == 0 and yl % 16 == 0 and nx == 128 and lax.axis_size("coil") == 2
+    return fast_body(*arrays) if fits else generic_body(*arrays)
 
 
 def solution(mesh):

time: 837 us -> 319 us (0.38); the launches traced: 826 us -> 317 us
  waiting for transfers between devices: 378 us -> 147 us
  local copies, waits for them, and re-layouts: 184 us -> 21.5 us
  matrix products: 151 us -> 16.2 us
  Pallas kernels: 0 us -> 63 us
  other arithmetic: 72.9 us -> 41.8 us
  between operations: 14.9 us -> 0.93 us
    dot_general x10 -> x6, matrix products: 151 us -> 16.2 us  [the longest x1 7.95 us: measured_images(): jnp.einsum('tpzqw,tkpzcx->kqwcx', tz, stacked, preferred_element_type=F32)]
    all_to_all x2, waiting for transfers between devices: 172 us -> 49.1 us  [the longest x1 49.1 us: fast_body(): lax.all_to_all(sent.astype(HALF), LINE, split_axis=0, concat_axis=0, tile...]
    ppermute x2, waiting for transfers between devices: 176 us -> 83.2 us  [extended(): before = lax.ppermute(last, axis, up)]
    pallas_call x0 -> x4, Pallas kernels: none -> 63 us  [the longest x1 20.5 us: regularizer(): pl.pallas_call(functools.partial(conv_kernel, nyb=nyb, hid=hid), in_specs...]
    dot_general x3 -> x0, local copies, waits for them, and re-layouts: 62.4 us -> none  [regularizer(): jnp.einsum('qc,czyx->qzyx', kernel_plane, framed_hidden[:, shift_z:shift_...]
    reshape x7 -> x2, local copies, waits for them, and re-layouts: 50.7 us -> 10.4 us  [the longest x1 10.4 us: measured_images(): return out.reshape(kyl, 2 * nz, nc * nx)]
    sub x7 -> x1, other arithmetic: 38.4 us -> 2.69 us  [fast_body(): return estimate - step_size[0] * (mine + received) - regular]
    all_gather x1 -> x0, waiting for transfers between devices: 27.9 us -> none  [body(): gathered = lax.all_gather(estimate, 'coil', axis=2, tiled=True)]
  transfers between devices with their start and end apart: 8 -> 8, of which waited for: 4 -> 4; matrix products, arithmetic and copies ran while one was open for 25% -> 15% of each run, Pallas kernels for 0% -> 6%
where the time goes in v1:
time: 319 us; the launch traced here: 317 us
  waiting for transfers between devices  147 us (46%)
  Pallas kernels  63 us (20%)
  other arithmetic  41.8 us (13%)
  starting transfers between devices  27 us (8%)
  local copies, waits for them, and re-layouts  21.5 us (7%)
  matrix products  16.2 us (5%)
    ppermute x2, waiting for transfers between devices, extended(): before = lax.ppermute(last, axis, up)  83.2 us
    all_to_all x1, waiting for transfers between devices, fast_body(): lax.all_to_all(sent.astype(HALF), LINE, split_axis=0, concat_axis=0, tile...  49.1 us
    pallas_call x1, Pallas kernels, regularizer(): pl.pallas_call(functools.partial(conv_kernel, nyb=nyb, hid=hid), in_specs...  20.5 us
    pallas_call x1, Pallas kernels, backward_y(): pl.pallas_call(backward_y_kernel, grid=(nc,), in_specs=[pl.BlockSpec((blo...  14.5 us
    pallas_call x1, Pallas kernels, forward_y(): pl.pallas_call(forward_y_kernel, grid=(nc,), in_specs=[pl.BlockSpec(memor...  14.4 us
    pallas_call x1, Pallas kernels, middle(): pl.pallas_call(middle_kernel, grid=(kyl // kb,), in_specs=[pl.BlockSpec(b...  13.6 us
    ppermute x1, waiting for transfers between devices, fast_body(): other = lax.ppermute(estimate.astype(HALF), 'coil', swap).astype(F32)  12.6 us
    reshape x1, local copies, waits for them, and re-layouts, measured_images(): return out.reshape(kyl, 2 * nz, nc * nx)  10.4 us
  transfers between devices with their start and end apart: 8, of which 4 were waited for; matrix products, arithmetic and copies ran while one was open for 15% of the time, Pallas kernels for 6%

profile of v1, /device:TPU:15, one launch (start us, length us, event | category | flops | bytes accessed | tf_op | source)
XLA Modules:
  0.0 317.2 jit_solution(15658478349223202111)
XLA Ops:
  0.0 1.8 fusion.30
  1.8 0.3 collective-permute-start
  2.1 12.6 %collective-permute-done = f16[2,16,64,128]{3,2,1,0:T(8,128)(2,1)S(1)} collective-permute-done((f16[2,16,64,128]{3,2,1,0:T(8,128)(2,1)S(1)}, f16[2,16,64,128]{3,2,1,0:T(8,128)(2,1)S(1)}, u32[]{:S(2)}, u32[]{:S(2)}) %collective-permute-start) | collective-permute-done | bytes 524320 | tf_op jit(solution)/shard_map/ppermute | solution.py:363
  14.7 1.1 convert_element_type.62.other_ref
  15.7 14.4 %forward_y.1 = f32[8,4,2,256,128]{4,3,2,1,0:T(8,128)} custom-call(s32[1]{0:T(128)} %bitcast.1.place_ref, f32[2,16,64,128]{3,2,1,0:T(8,128)} %own_ref.1, f32[2,16,64,128]{3,2,1,0:T(8,128)} %convert_element_type.62.other_ref, bf16[2,4,16,128,128]{4,3,2,1,0:T(8,128)(2,1)} %sens_ref.3, bf16[2,256,256]{2,1,0:T(8,128)(2,1)} %constant.50.clone.table_ref), custom_call_target="tpu_custom_call" | custom-call | flops 3221225472 | bytes 14680064 | tf_op jit(solution)/shard_map/forward_y/pallas_call | solution.py:79
  30.1 6.4 %convert_element_type.63 = f16[8,4,2,256,128]{4,3,2,1,0:T(8,128)(2,1)} convert(f32[8,4,2,256,128]{4,3,2,1,0:T(8,128)} %forward_y.1) | non-fusion elementwise | flops 2097152 | bytes 12582912 | tf_op jit(solution)/shard_map/convert_element_type | solution.py:367
  36.5 6.6 %all-to-all-start = ((f16[8,4,2,256,128]{4,3,2,1,0:T(8,128)(2,1)}), f16[8,4,2,256,128]{4,3,2,1,0:T(8,128)(2,1)}, u32[]{:S(2)}, u32[]{:S(2)}) async-start(f16[8,4,2,256,128]{4,3,2,1,0:T(8,128)(2,1)} %convert_element_type.63), calls=%async_computation | async-start | bytes 8388608 | tf_op jit(solution)/shard_map/all_to_all | solution.py:367
  43.1 0.0 copy-done.7
  43.1 0.1 copy.33
  43.2 2.5 select_bitcast_fusion
  45.8 0.0 copy-done.4
  45.8 0.0 copy-start.3
  45.8 1.6 fusion.8
  47.4 0.0 copy-done.3
  47.5 0.0 copy-start.14
  47.5 4.2 %fusion.6 = (bf16[1,16,2,128,4,128]{5,3,2,1,4,0:T(8,128)(2,1)S(1)}, bf16[1,16,2,128,4,128]{5,3,2,1,4,0:T(8,128)(2,1)}) fusion(f32[4,128,16,2,128,1]{4,1,5,3,2,0:T(8,128)S(1)} %fusion.8, bf16[2,128,2,128,1,1]{3,1,0,2,5,4:T(8,128)(2,1)S(1)} %copy-done.3, bf16[2,4,128,16,128,1]{4,3,2,1,0,5:T(8,128)(2,1)S(1)} %select_bitcast_fusion), kind=kOutput, calls=%fused_computation.12 | convolution fusion | flops 1084227584 | bytes 21102592 | tf_op jit(solution)/shard_map/pfqx,pczkf->kqzcx/dot_general | solution.py:198
  51.7 0.0 copy-done.14
  51.7 7.9 %fusion.12 = f32[16,2,128,4,128]{2,4,3,0,1:T(8,128)} fusion(bf16[3,2,128,2,128,1,1]{4,2,1,6,5,3,0:T(8,128)(2,1)S(1)} %copy-done.14, bf16[1,16,2,128,4,128]{5,3,2,1,4,0:T(8,128)(2,1)} %get-tuple-element.6, bf16[1,16,2,128,4,128]{5,3,2,1,4,0:T(8,128)(2,1)S(1)} %get-tuple-element.5), kind=kOutput, calls=%fused_computation.21 | convolution fusion | flops 3233808384 | bytes 17170432 | tf_op jit(solution)/shard_map/tpzqw,tkpzcx->kqwcx/dot_general | solution.py:207
  59.6 9.9 %copy.37 = f32[16,2,128,4,128]{4,3,2,1,0:T(4,128)} copy(f32[16,2,128,4,128]{2,4,3,0,1:T(8,128)} %fusion.12) | data formatting | bytes 16777216 | tf_op jit(solution)/shard_map/tpzqw,tkpzcx->kqwcx/transpose | solution.py:207
  69.5 10.4 %reshape.39.meas_ref = f32[16,256,512]{2,1,0:T(8,128)} reshape(f32[16,2,128,4,128]{4,3,2,1,0:T(4,128)} %copy.37) | data formatting | bytes 16777216 | tf_op jit(solution)/shard_map/reshape | solution.py:208
  80.0 0.0 copy-done.12
  80.0 0.0 copy-done.13
  80.0 2.0 fusion.18
  82.1 2.4 pad_maximum_fusion.circ_ref
  84.4 49.1 %all-to-all-done = f16[8,4,2,256,128]{4,3,2,1,0:T(8,128)(2,1)} async-done(((f16[8,4,2,256,128]{4,3,2,1,0:T(8,128)(2,1)}), f16[8,4,2,256,128]{4,3,2,1,0:T(8,128)(2,1)}, u32[]{:S(2)}, u32[]{:S(2)}) %all-to-all-start) | async-done | bytes 4194336 | tf_op jit(solution)/shard_map/all_to_all | solution.py:367
  133.6 6.2 %convert_element_type.64.in_ref = f32[8,4,2,256,128]{4,3,2,1,0:T(8,128)} convert(f16[8,4,2,256,128]{4,3,2,1,0:T(8,128)(2,1)} %all-to-all-done) | non-fusion elementwise | flops 2097152 | bytes 12582912 | tf_op jit(solution)/shard_map/convert_element_type | solution.py:370
  139.7 13.6 %middle_z.1 = f32[8,4,2,256,128]{4,3,2,1,0:T(8,128)} custom-call(f32[8,4,2,256,128]{4,3,2,1,0:T(8,128)} %convert_element_type.64.in_ref, bf16[2,16,256,256]{3,2,1,0:T(8,128)(2,1)} %pad_maximum_fusion.circ_ref, f32[16,256,512]{2,1,0:T(8,128)} %reshape.39.meas_ref), custom_call_target="tpu_custom_call" | custom-call | flops 3221225472 | bytes 25165824 | tf_op jit(solution)/shard_map/middle_z/pallas_call | solution.py:125
  153.3 6.3 %convert_element_type.69 = f16[8,4,2,256,128]{4,3,2,1,0:T(8,128)(2,1)} convert(f32[8,4,2,256,128]{4,3,2,1,0:T(8,128)} %middle_z.1) | non-fusion elementwise | flops 2097152 | bytes 12582912 | tf_op jit(solution)/shard_map/convert_element_type | solution.py:372
  159.7 0.0 copy-start.6
  159.7 0.0 copy-start.5
  159.7 0.0 copy-start.11
  159.7 8.3 %all-to-all-start.1 = ((f16[8,4,2,256,128]{4,3,2,1,0:T(8,128)(2,1)}), f16[8,4,2,256,128]{4,3,2,1,0:T(8,128)(2,1)}, u32[]{:S(2)}, u32[]{:S(2)}) async-start(f16[8,4,2,256,128]{4,3,2,1,0:T(8,128)(2,1)} %convert_element_type.69), calls=%async_computation.1 | async-start | bytes 8388608 | tf_op jit(solution)/shard_map/all_to_all | solution.py:372
  168.0 3.4 %collective-permute-start.2 = (bf16[2,2,64,128]{3,2,1,0:T(8,128)(2,1)S(1)}, bf16[2,2,64,128]{3,2,1,0:T(8,128)(2,1)S(1)}, u32[]{:S(2)}, u32[]{:S(2)}) collective-permute-start(bf16[2,2,64,128]{3,2,1,0:T(8,128)(2,1)S(1)} %get-tuple-element.13), channel_id=1, source_target_pairs={{0,1},{1,4},{4,5},{5,8},{8,9},{9,12},{12,13},{2,3},{3,6},{6,7},{7,... | collective-permute-start | bytes 196616 | tf_op jit(solution)/shard_map/ppermute | solution.py:345
  171.3 1.9 collective-permute-start.3
  173.3 0.0 copy-done.10
  173.3 0.0 copy-done.9
  173.4 0.0 copy-done.8
  173.4 0.2 convolution_bitcast_fusion
  173.6 0.0 copy-done.2
  173.6 1.2 multiply_reduce_fusion
  174.8 0.0 copy-done.6
  174.8 0.1 convolution_bitcast_fusion.1
  174.9 0.0 copy-done.5
  175.0 0.9 multiply_reduce_fusion.1
  175.9 83.2 %collective-permute-done.2 = bf16[2,2,64,128]{3,2,1,0:T(8,128)(2,1)S(1)} collective-permute-done((bf16[2,2,64,128]{3,2,1,0:T(8,128)(2,1)S(1)}, bf16[2,2,64,128]{3,2,1,0:T(8,128)(2,1)S(1)}, u32[]{:S(2)}, u32[]{:S(2)}) %collective-permute-start.2) | collective-permute-done | bytes 65568 | tf_op jit(solution)/shard_map/ppermute | solution.py:345
  259.1 1.8 collective-permute-done.3
  260.9 1.3 collective-permute-start.4
  262.2 4.2 %collective-permute-start.5 = (bf16[2,20,2,128]{3,2,1,0:T(2,128)(2,1)S(1)}, bf16[2,20,2,128]{3,2,1,0:T(2,128)(2,1)S(1)}, u32[]{:S(2)}, u32[]{:S(2)}) collective-permute-start(bf16[2,20,2,128]{3,2,1,0:T(2,128)(2,1)S(1)} %get-tuple-element.12), channel_id=1, source_target_pairs={{2,0},{3,1},{6,4},{7,5},{10,8},{11,9},{14,12},{15,13},{18,16},{19,... | collective-permute-start | bytes 61448 | tf_op jit(solution)/shard_map/ppermute | solution.py:346
  266.4 0.6 pad_add_fusion.edge_ref
  267.0 0.0 copy-done.11
  267.0 0.1 broadcast_in_dim.25
  267.7 0.0 collective-permute-done.4
  267.7 0.0 collective-permute-done.5
  267.7 1.4 fusion.26.frame_ref
  269.2 0.0 all-to-all-done.1
  269.2 6.2 %convert_element_type.70.in_ref = f32[8,4,2,256,128]{4,3,2,1,0:T(8,128)} convert(f16[8,4,2,256,128]{4,3,2,1,0:T(8,128)(2,1)} %all-to-all-done.1) | non-fusion elementwise | flops 2097152 | bytes 12582912 | tf_op jit(solution)/shard_map/convert_element_type | solution.py:373
  275.4 14.5 %backward_y.1 = f32[2,16,128,128]{3,2,1,0:T(8,128)} custom-call(f32[8,4,2,256,128]{4,3,2,1,0:T(8,128)} %convert_element_type.70.in_ref, bf16[2,4,16,128,128]{4,3,2,1,0:T(8,128)(2,1)} %sens_ref.3, bf16[2,256,256]{2,1,0:T(8,128)(2,1)} %constant.51.clone.table_ref), custom_call_target="tpu_custom_call" | custom-call | flops 3221225472 | bytes 14680064 | tf_op jit(solution)/shard_map/backward_y/pallas_call | solution.py:176
  289.9 2.2 multiply_convert_fusion
  292.1 1.1 collective-permute-start.1
  293.2 0.8 broadcast_in_dim.26.bias_ref
  294.0 20.5 %regularizer.1 = f32[2,16,64,128]{3,2,1,0:T(8,128)} custom-call(s32[4]{0:T(128)} %pad_add_fusion.edge_ref, f32[2,20,72,128]{3,2,1,0:T(8,128)} %fusion.26.frame_ref, bf16[576,432]{1,0:T(8,128)(2,1)} %bitcast.85, bf16[288,576]{1,0:T(8,128)(2,1)} %bitcast.86, f32[576,128]{1,0:T(8,128)} %broadcast_in_dim.26.bias_ref), custom_call_target="tpu_custom_call" | custom-call | flops 7644119040 | bytes 4194304 | tf_op jit(solution)/shard_map/regularizer/pallas_call | solution.py:322
  314.5 0.0 collective-permute-done.1
  314.5 0.0 copy-done.1
  314.5 2.7 subtract_subtract_fusion
  (22 shorter events, 0.2 us)
Async XLA Ops:
  1.8 12.9 %collective-permute-start = (f16[2,16,64,128]{3,2,1,0:T(8,128)(2,1)S(1)}, f16[2,16,64,128]{3,2,1,0:T(8,128)(2,1)S(1)}, u32[]{:S(2)}, u32[]{:S(2)}) collective-permute-start(f16[2,16,64,128]{3,2,1,0:T(8,128)(2,1)S(1)} %get-tuple-element.9), channel_id=1, source_target_pairs={{0,2},{2,0},{1,3},{3,1},{4,6},{6,4},{5,7},{7,5},{8,10},{10,8},{9,1... | collective-permute-start | bytes 1572872 | tf_op jit(solution)/shard_map/ppermute | solution.py:363
  36.5 6.6 %copy-start.7 = (s32[128,16]{0,1:T(8,128)S(1)}, s32[128,16]{0,1:T(8,128)}, u32[]{:S(2)}) copy-start(s32[128,16]{0,1:T(8,128)} %param.19) | copy-start | bytes 24580
  36.5 97.1 %all-to-all-start = ((f16[8,4,2,256,128]{4,3,2,1,0:T(8,128)(2,1)}), f16[8,4,2,256,128]{4,3,2,1,0:T(8,128)(2,1)}, u32[]{:S(2)}, u32[]{:S(2)}) async-start(f16[8,4,2,256,128]{4,3,2,1,0:T(8,128)(2,1)} %convert_element_type.63), calls=%async_computation | async-start | bytes 8388608 | tf_op jit(solution)/shard_map/all_to_all | solution.py:367
  43.2 2.6 copy-start.4
  45.8 1.7 copy-start.3
  47.5 4.2 %copy-start.14 = (bf16[3,2,128,2,128,1,1]{4,2,1,6,5,3,0:T(8,128)(2,1)S(1)}, bf16[3,2,128,2,128,1,1]{4,2,1,6,5,3,0:T(8,128)(2,1)}, u32[]{:S(2)}) copy-start(bf16[3,2,128,2,128,1,1]{4,2,1,6,5,3,0:T(8,128)(2,1)} %constant.74) | copy-start | bytes 1179652
  69.5 10.5 %copy-start.12 = (bf16[768,256]{0,1:T(8,128)(2,1)S(1)}, bf16[768,256]{0,1:T(8,128)(2,1)}, u32[]{:S(2)}) copy-start(bf16[768,256]{0,1:T(8,128)(2,1)} %constant.62) | copy-start | bytes 1179652
  69.5 10.5 %copy-start.13 = (bf16[768,256,1]{1,0,2:T(8,128)(2,1)S(1)}, bf16[768,256,1]{1,0,2:T(8,128)(2,1)}, u32[]{:S(2)}) copy-start(bf16[768,256,1]{1,0,2:T(8,128)(2,1)} %constant.71) | copy-start | bytes 1179652
  159.6 13.6 %copy-start.10 = (bf16[32,2,3,3,3]{0,1,4,3,2:T(2,128)(2,1)S(1)}, bf16[32,2,3,3,3]{0,1,4,3,2:T(2,128)(2,1)}, u32[]{:S(2)}) copy-start(bf16[32,2,3,3,3]{0,1,4,3,2:T(2,128)(2,1)} %param.21) | copy-start | bytes 10372
  159.6 13.7 %copy-start.9 = (bf16[2,32,3,3,3]{1,0,4,3,2:T(2,128)(2,1)S(1)}, bf16[2,32,3,3,3]{1,0,4,3,2:T(2,128)(2,1)}, u32[]{:S(2)}) copy-start(bf16[2,32,3,3,3]{1,0,4,3,2:T(2,128)(2,1)} %param.23) | copy-start | bytes 10372
  159.6 13.7 %copy-start.8 = (bf16[18,432,1]{1,0,2:T(8,128)(2,1)S(1)}, bf16[18,432,1]{1,0,2:T(8,128)(2,1)}, u32[]{:S(2)}) copy-start(bf16[18,432,1]{1,0,2:T(8,128)(2,1)} %constant.75) | copy-start | bytes 46660
  159.6 13.9 %copy-start.2 = (f32[3,18,432]{2,1,0:T(8,128)S(1)}, f32[3,18,432]{2,1,0:T(8,128)}, u32[]{:S(2)}) copy-start(f32[3,18,432]{2,1,0:T(8,128)} %constant.69) | copy-start | bytes 279940
  159.7 15.1 %copy-start.6 = (bf16[32,576,1]{1,0,2:T(8,128)(2,1)S(1)}, bf16[32,576,1]{1,0,2:T(8,128)(2,1)}, u32[]{:S(2)}) copy-start(bf16[32,576,1]{1,0,2:T(8,128)(2,1)} %constant.76) | copy-start | bytes 110596
  159.7 15.3 %copy-start.5 = (f32[3,16,576]{2,1,0:T(8,128)S(1)}, f32[3,16,576]{2,1,0:T(8,128)}, u32[]{:S(2)}) copy-start(f32[3,16,576]{2,1,0:T(8,128)} %constant.70) | copy-start | bytes 331780
  159.7 107.3 %copy-start.11 = (f32[32]{0:T(128)S(1)}, f32[32]{0:T(128)}, u32[]{:S(2)}) copy-start(f32[32]{0:T(128)} %param.22) | copy-start | bytes 388
  159.7 109.5 %all-to-all-start.1 = ((f16[8,4,2,256,128]{4,3,2,1,0:T(8,128)(2,1)}), f16[8,4,2,256,128]{4,3,2,1,0:T(8,128)(2,1)}, u32[]{:S(2)}, u32[]{:S(2)}) async-start(f16[8,4,2,256,128]{4,3,2,1,0:T(8,128)(2,1)} %convert_element_type.69), calls=%async_computation.1 | async-start | bytes 8388608 | tf_op jit(solution)/shard_map/all_to_all | solution.py:372
  168.0 91.1 %collective-permute-start.2 = (bf16[2,2,64,128]{3,2,1,0:T(8,128)(2,1)S(1)}, bf16[2,2,64,128]{3,2,1,0:T(8,128)(2,1)S(1)}, u32[]{:S(2)}, u32[]{:S(2)}) collective-permute-start(bf16[2,2,64,128]{3,2,1,0:T(8,128)(2,1)S(1)} %get-tuple-element.13), channel_id=1, source_target_pairs={{0,1},{1,4},{4,5},{5,8},{8,9},{9,12},{12,13},{2,3},{3,6},{6,7},{7,... | collective-permute-start | bytes 196616 | tf_op jit(solution)/shard_map/ppermute | solution.py:345
  171.3 89.5 %collective-permute-start.3 = (bf16[2,2,64,128]{3,2,1,0:T(8,128)(2,1)S(1)}, bf16[2,2,64,128]{3,2,1,0:T(8,128)(2,1)S(1)}, u32[]{:S(2)}, u32[]{:S(2)}) collective-permute-start(bf16[2,2,64,128]{3,2,1,0:T(8,128)(2,1)S(1)} %get-tuple-element.14), channel_id=1, source_target_pairs={{1,0},{4,1},{5,4},{8,5},{9,8},{12,9},{13,12},{3,2},{6,3},{7,6},{10... | collective-permute-start | bytes 196616 | tf_op jit(solution)/shard_map/ppermute | solution.py:346
  260.9 6.8 %collective-permute-start.4 = (bf16[2,20,2,128]{3,2,1,0:T(2,128)(2,1)S(1)}, bf16[2,20,2,128]{3,2,1,0:T(2,128)(2,1)S(1)}, u32[]{:S(2)}, u32[]{:S(2)}) collective-permute-start(bf16[2,20,2,128]{3,2,1,0:T(2,128)(2,1)S(1)} %get-tuple-element.11), channel_id=1, source_target_pairs={{0,2},{1,3},{4,6},{5,7},{8,10},{9,11},{12,14},{13,15},{16,18},{17,... | collective-permute-start | bytes 61448 | tf_op jit(solution)/shard_map/ppermute | solution.py:345
  262.2 5.5 %collective-permute-start.5 = (bf16[2,20,2,128]{3,2,1,0:T(2,128)(2,1)S(1)}, bf16[2,20,2,128]{3,2,1,0:T(2,128)(2,1)S(1)}, u32[]{:S(2)}, u32[]{:S(2)}) collective-permute-start(bf16[2,20,2,128]{3,2,1,0:T(2,128)(2,1)S(1)} %get-tuple-element.12), channel_id=1, source_target_pairs={{2,0},{3,1},{6,4},{7,5},{10,8},{11,9},{14,12},{15,13},{18,16},{19,... | collective-permute-start | bytes 61448 | tf_op jit(solution)/shard_map/ppermute | solution.py:346
  292.1 22.4 %collective-permute-start.1 = (f16[2,16,64,128]{3,2,1,0:T(8,128)(2,1)}, f16[2,16,64,128]{3,2,1,0:T(8,128)(2,1)}, u32[]{:S(2)}, u32[]{:S(2)}) collective-permute-start(f16[2,16,64,128]{3,2,1,0:T(8,128)(2,1)} %multiply_convert_fusion), channel_id=1, source_target_pairs={{0,2},{2,0},{1,3},{3,1},{4,6},{6,4},{5,7},{7,5},{8,10},{10,8},{9,1... | collective-permute-start | bytes 1572872 | tf_op jit(solution)/shard_map/ppermute | solution.py:376
  294.0 20.5 %copy-start = (f32[2,16,64,128]{3,2,1,0:T(8,128)S(1)}, f32[2,16,64,128]{3,2,1,0:T(8,128)}, u32[]{:S(2)}) copy-start(f32[2,16,64,128]{3,2,1,0:T(8,128)} %own_ref.1) | copy-start | bytes 3145732
  294.0 20.5 %copy-start.1 = (f32[2,16,128,128]{3,2,1,0:T(8,128)S(1)}, f32[2,16,128,128]{3,2,1,0:T(8,128)}, u32[]{:S(2)}) copy-start(f32[2,16,128,128]{3,2,1,0:T(8,128)} %backward_y.1) | copy-start | bytes 6291460

commit v2 on v1

--- a/solution.py
+++ b/solution.py
@@ -9,11 +9,13 @@
 from jax.experimental.pallas import tpu as pltpu
 from jax.sharding import PartitionSpec as P
 
+
 LINE = ("slab", "pencil")
 HALF = jnp.float16
 F32 = jnp.float32
 BF16 = jnp.bfloat16
 SCALE = 1.0 / 16.0
+CHUNKS = 2
 
 
 def line_dft(n):
@@ -36,21 +38,64 @@
 def dot3(table, data):
     high = data.astype(BF16)
     low = (data - high.astype(F32)).astype(BF16)
-    return dot(table[0], high) + dot(table[1], high) + dot(table[0], low)
-
-
-def forward_y_kernel(place_ref, own_ref, other_ref, sens_ref, table_ref, out_ref):
+    return dot(table, jnp.concatenate([high, high, low], axis=0))
+
+
+def wide(table):
+    return jnp.concatenate([table[0], table[1], table[0]], axis=1)
+
+
+def by_device(table, slabs, cores):
+    _, rows, columns = table.shape
+    width = rows // (2 * slabs * cores)
+    table = jnp.asarray(table).reshape(4, slabs, cores, width, columns)
+    for axis, name, size in ((1, "slab", slabs), (2, "pencil", cores)):
+        at = lax.axis_index(name)
+        for bit in range(size.bit_length() - 1):
+            other = np.arange(size) ^ (1 << bit)
+            flipped = jnp.concatenate([lax.slice_in_dim(table, o, o + 1, axis=axis) for o in other], axis=axis)
+            table = jnp.where((at >> bit) & 1 == 1, flipped, table)
+    return table.reshape(2, rows, columns)
+
+
+def payloads(near, far, slabs):
+    got = lax.ppermute(far.astype(HALF), "pencil", [(0, 1), (1, 0)])
+    both = [jnp.stack([near[k].astype(HALF), got[k]]) for k in range(slabs - 1, 0, -1)]
+    return both, [near, got[0].astype(F32)[None]]
+
+
+def delivered(both, own, slabs):
+    moved = {}
+    for k, payload in zip(range(slabs - 1, 0, -1), both):
+        moved[k] = lax.ppermute(payload, "slab", [(i, i ^ k) for i in range(slabs)])
+        moved[k] = moved[k].astype(F32)
+    return own + [moved[k] for k in range(1, slabs)]
+
+
+def piece_specs(pieces, block, index):
+    specs = []
+    for k, piece in enumerate(pieces):
+        lead = 1 if k < 2 else piece.shape[0]
+        specs.append(pl.BlockSpec((lead,) + block, index))
+    return specs
+
+
+def piece_views(refs):
+    return [ref.at[lead] for ref in refs for lead in range(ref.shape[0])]
+
+
+def forward_y_kernel(place_ref, own_ref, other_ref, sens_ref, table_ref, near_ref, far_ref):
     first = place_ref[0] == 0
     zl = own_ref.shape[1]
-    blocks = out_ref.shape[0]
-    kyl = out_ref.shape[3] // zl
+    slabs = near_ref.shape[0]
+    kyl = near_ref.shape[3] // zl
     n = 2 * own_ref.shape[2]
-    table = (table_ref[0], table_ref[1])
+    table = table_ref[...]
 
     def image(z):
         parts = []
         for ri in range(2):
-            own, other = own_ref[ri, z], other_ref[ri, z].astype(F32)
+            own, other = own_ref[ri, z], other_ref[ri, z]
             top = jnp.where(first, own, other)
             bottom = jnp.where(first, other, own)
             parts.append(jnp.concatenate([top, bottom], axis=0))
@@ -64,18 +109,21 @@
         result = dot3(table, data)
         x = result.shape[1] // 2
         for half in range(2):
-            for d in range(blocks):
-                for ro in range(2):
-                    rows = result[ro * n + d * kyl : ro * n + (d + 1) * kyl, half * x : (half + 1) * x]
-                    out_ref[d, 0, ro, pl.ds(2 * p + half, kyl, stride=zl), :] = rows
+            for k in range(slabs):
+                for core, ref in enumerate((near_ref, far_ref)):
+                    d = 2 * k + core
+                    for ro in range(2):
+                        rows = result[ro * n + d * kyl : ro * n + (d + 1) * kyl, half * x : (half + 1) * x]
+                        ref[k, 0, ro, pl.ds(2 * p + half, kyl, stride=zl), :] = rows
         return carry
 
     lax.fori_loop(0, zl // 2, step, 0)
 
 
-def forward_y(place, own, other, sens, table, blocks):
-    _, nc, zl, n, x = sens.shape
-    kyl = n // blocks
+def forward_y(place, own, other, sens, table, slabs, first, nc):
+    _, _, zl, n, x = sens.shape
+    kyl = n // (2 * slabs)
+    out = pl.BlockSpec((slabs, 1, 2, kyl * zl, x), lambda c: (0, c, 0, 0, 0))
     return pl.pallas_call(
         forward_y_kernel,
         grid=(nc,),
@@ -83,79 +131,81 @@
             pl.BlockSpec(memory_space=pltpu.SMEM),
             pl.BlockSpec(own.shape, lambda c: (0, 0, 0, 0)),
             pl.BlockSpec(other.shape, lambda c: (0, 0, 0, 0)),
-            pl.BlockSpec((2, 1, zl, n, x), lambda c: (0, c, 0, 0, 0)),
-            pl.BlockSpec(table.shape, lambda c: (0, 0, 0)),
+            pl.BlockSpec((2, 1, zl, n, x), lambda c: (0, first + c if first else c, 0, 0, 0)),
+            pl.BlockSpec(table.shape, lambda c: (0, 0)),
         ],
-        out_specs=pl.BlockSpec((blocks, 1, 2, kyl * zl, x), lambda c: (0, c, 0, 0, 0)),
-        out_shape=jax.ShapeDtypeStruct((blocks, nc, 2, kyl * zl, x), F32),
+        out_specs=[out, out],
+        out_shape=[jax.ShapeDtypeStruct((slabs, nc, 2, kyl * zl, x), F32)] * 2,
         cost_estimate=pl.CostEstimate(
-            flops=2 * 3 * 2 * n * 2 * n * nc * zl * x, bytes_accessed=14 * sens.size // 2, transcendentals=0
+            flops=2 * 3 * 2 * n * 2 * n * nc * zl * x, bytes_accessed=14 * nc * zl * n * x, transcendentals=0
         ),
-        name="forward_y",
     )(place, own, other, sens, table)
 
 
-def middle_kernel(in_ref, circ_ref, meas_ref, out_ref):
-    blocks, nc = in_ref.shape[0], in_ref.shape[1]
-    kys = circ_ref.shape[1]
-    zl = in_ref.shape[3] // kys
-    x = in_ref.shape[4]
-    n = blocks * zl
+def middle_kernel(count, *refs):
+    pieces = piece_views(refs[:count])
+    high_ref, low_ref, meas_ref, near_ref, far_ref = refs[count:]
+    nc = pieces[0].shape[0]
+    kys = high_ref.shape[0]
+    zl = pieces[0].shape[2] // kys
+    x = pieces[0].shape[3]
+    n = len(pieces) * zl
     for k in range(kys):
         columns = []
         for c in range(nc):
-            rows = [in_ref[s, c, ri, k * zl : (k + 1) * zl, :] for ri in range(2) for s in range(blocks)]
+            rows = [piece[c, ri, k * zl : (k + 1) * zl, :] for ri in range(2) for piece in pieces]
             columns.append(jnp.concatenate(rows, axis=0))
         data = jnp.concatenate(columns, axis=1)
-        result = dot3((circ_ref[0, k], circ_ref[1, k]), data) - meas_ref[k]
+        table = jnp.concatenate([high_ref[k], low_ref[k], high_ref[k]], axis=1)
+        result = dot3(table, data) - meas_ref[k]
         for c in range(nc):
             for ri in range(2):
-                for d in range(blocks):
-                    out_ref[d, c, ri, k * zl : (k + 1) * zl, :] = result[
+                for d in range(len(pieces)):
+                    ref = far_ref if d % 2 else near_ref
+                    ref[d // 2, c, ri, k * zl : (k + 1) * zl, :] = result[
                         ri * n + d * zl : ri * n + (d + 1) * zl, c * x : (c + 1) * x
                     ]
 
 
-def middle(data, circ, meas):
-    blocks, nc, _, rows, x = data.shape
-    kyl, n2 = circ.shape[1], circ.shape[2]
+def middle(pieces, circ, meas):
+    _, nc, _, rows, x = pieces[0].shape
+    kyl, n2 = circ[0].shape[:2]
     zl = rows // kyl
+    slabs = n2 // (4 * zl)
     kb = 2
-    block = (blocks, nc, 2, kb * zl, x)
+    out = pl.BlockSpec((slabs, nc, 2, kb * zl, x), lambda k: (0, 0, 0, k, 0))
     return pl.pallas_call(
-        middle_kernel,
+        functools.partial(middle_kernel, len(pieces)),
         grid=(kyl // kb,),
-        in_specs=[
-            pl.BlockSpec(block, lambda k: (0, 0, 0, k, 0)),
-            pl.BlockSpec((2, kb, n2, n2), lambda k: (0, k, 0, 0)),
+        in_specs=piece_specs(pieces, (nc, 2, kb * zl, x), lambda k: (0, 0, 0, k, 0))
+        + [
+            pl.BlockSpec((kb, n2, n2), lambda k: (k, 0, 0)),
+            pl.BlockSpec((kb, n2, n2), lambda k: (k, 0, 0)),
             pl.BlockSpec((kb, n2, nc * x), lambda k: (k, 0, 0)),
         ],
-        out_specs=pl.BlockSpec(block, lambda k: (0, 0, 0, k, 0)),
-        out_shape=jax.ShapeDtypeStruct(data.shape, F32),
+        out_specs=[out, out],
+        out_shape=[jax.ShapeDtypeStruct((slabs, nc, 2, rows, x), F32)] * 2,
         cost_estimate=pl.CostEstimate(
-            flops=2 * 3 * n2 * n2 * kyl * nc * x, bytes_accessed=12 * data.size, transcendentals=0
+            flops=2 * 3 * n2 * n2 * kyl * nc * x, bytes_accessed=12 * nc * n2 * kyl * x, transcendentals=0
         ),
-        name="middle_z",
-    )(data, circ, meas)
-
-
-def backward_y_kernel(in_ref, sens_ref, table_ref, out_ref):
-    blocks = in_ref.shape[0]
-    zl = out_ref.shape[1]
-    n, x = out_ref.shape[2], out_ref.shape[3]
-    kyl = n // blocks
-    table = (table_ref[0], table_ref[1])
+    )(*pieces, *circ, meas)
+
+
+def backward_y_kernel(count, *refs):
+    pieces = piece_views(refs[:count])
+    sens_ref, table_ref, before_ref, out_ref = refs[count:]
+    zl, n, x = out_ref.shape[1:]
+    kyl = n // len(pieces)
+    table = table_ref[...]
 
     @pl.when(pl.program_id(0) == 0)
     def _():
-        out_ref[...] = jnp.zeros_like(out_ref)
+        out_ref[...] = before_ref[...]
 
     def step(p, carry):
         columns = []
         for half in range(2):
-            rows = [
-                in_ref[s, 0, ri, pl.ds(2 * p + half, kyl, stride=zl), :] for ri in range(2) for s in range(blocks)
-            ]
+            rows = [piece[0, ri, pl.ds(2 * p + half, kyl, stride=zl), :] for ri in range(2) for piece in pieces]
             columns.append(jnp.concatenate(rows, axis=0))
         result = dot3(table, jnp.concatenate(columns, axis=1))
         for half in range(2):
@@ -170,54 +220,70 @@
     lax.fori_loop(0, zl // 2, step, 0)
 
 
-def backward_y(data, sens, table):
-    _, nc, zl, n, x = sens.shape
-    blocks = data.shape[0]
+def backward_y(pieces, sens, table, before, first):
+    _, _, zl, n, x = sens.shape
+    _, nc, _, rows, _ = pieces[0].shape
+    whole = pl.BlockSpec((2, zl, n, x), lambda c: (0, 0, 0, 0))
     return pl.pallas_call(
-        backward_y_kernel,
+        functools.partial(backward_y_kernel, len(pieces)),
         grid=(nc,),
-        in_specs=[
-            pl.BlockSpec((blocks, 1, 2, data.shape[3], x), lambda c: (0, c, 0, 0, 0)),
-            pl.BlockSpec((2, 1, zl, n, x), lambda c: (0, c, 0, 0, 0)),
-            pl.BlockSpec(table.shape, lambda c: (0, 0, 0)),
+        in_specs=piece_specs(pieces, (1, 2, rows, x), lambda c: (0, c, 0, 0, 0))
+        + [
+            pl.BlockSpec((2, 1, zl, n, x), lambda c: (0, first + c if first else c, 0, 0, 0)),
+            pl.BlockSpec(table.shape, lambda c: (0, 0)),
+            whole,
         ],
-        out_specs=pl.BlockSpec((2, zl, n, x), lambda c: (0, 0, 0, 0)),
+        out_specs=whole,
         out_shape=jax.ShapeDtypeStruct((2, zl, n, x), F32),
+        input_output_aliases={len(pieces) + 2: 0},
         cost_estimate=pl.CostEstimate(
-            flops=2 * 3 * 2 * n * 2 * n * nc * zl * x, bytes_accessed=14 * sens.size // 2, transcendentals=0
+            flops=2 * 3 * 2 * n * 2 * n * nc * zl * x, bytes_accessed=14 * nc * zl * n * x, transcendentals=0
         ),
-        name="backward_y",
-    )(data, sens, table)
-
-
-def measured_images(measured, sampling, table_z, table_x):
-    _, nc, nz, kyl, nx = measured.shape
+    )(*pieces, sens, table, before)
+
+
+def measured_kernel(high_ref, low_ref, table_ref, out_ref):
+    nc, kys = high_ref.shape[:2]
+    for k in range(kys):
+        high = jnp.concatenate([high_ref[c, k] for c in range(nc)], axis=1)
+        low = jnp.concatenate([low_ref[c, k] for c in range(nc)], axis=1)
+        out_ref[k] = dot(table_ref[...], jnp.concatenate([high, high, low], axis=0))
+
+
+def measured_images(measured, sampling, table_x, back_z, first, nc):
+    measured = lax.slice_in_dim(measured, first, first + nc, axis=1)
+    _, _, nz, kyl, nx = measured.shape
     masked = jnp.where((sampling > 0)[None, None, :, :, None], measured, 0).astype(BF16)
-    tx = table_x.reshape(2, 2, nx, 2, nx)
-    form = "pfqx,pczkf->kqzcx"
+    tx = jnp.asarray(table_x).reshape(2, 2, nx, 2, nx)
+    form = "pfqx,pczkf->ckqzx"
     along_x = jnp.einsum(form, tx[0], masked, preferred_element_type=F32)
     along_x = along_x + jnp.einsum(form, tx[1], masked, preferred_element_type=F32)
     high = lax.reduce_precision(along_x, 8, 7)
-    low = (along_x - high).astype(BF16)
-    high = high.astype(BF16)
-    stacked = jnp.stack([high, low])
-    tz = table_z.reshape(2, 2, nz, 2, nz)
-    tz = jnp.stack([tz[0], tz[0], tz[1]])
-    stacked = jnp.stack([high, low, high])
-    out = jnp.einsum("tpzqw,tkpzcx->kqwcx", tz, stacked, preferred_element_type=F32)
-    return out.reshape(kyl, 2 * nz, nc * nx)
-
-
-def circulants(sampling, table_z):
-    nz = sampling.shape[0]
+    low = (along_x - high).astype(BF16).reshape(nc, kyl, 2 * nz, nx)
+    high = high.astype(BF16).reshape(nc, kyl, 2 * nz, nx)
+    kb = 2
+    block = pl.BlockSpec((nc, kb, 2 * nz, nx), lambda k: (0, k, 0, 0))
+    return pl.pallas_call(
+        measured_kernel,
+        grid=(kyl // kb,),
+        in_specs=[block, block, pl.BlockSpec(back_z.shape, lambda k: (0, 0))],
+        out_specs=pl.BlockSpec((kb, 2 * nz, nc * nx), lambda k: (k, 0, 0)),
+        out_shape=jax.ShapeDtypeStruct((kyl, 2 * nz, nc * nx), F32),
+        cost_estimate=pl.CostEstimate(
+            flops=2 * 3 * 4 * nz * nz * kyl * nc * nx, bytes_accessed=16 * nc * kyl * nz * nx, transcendentals=0
+        ),
+    )(high, low, back_z)
+
+
+def circulants(sampling, back_z):
     weights = (sampling > 0).astype(BF16).T
     weights = jnp.concatenate([weights, weights], axis=1)
-    left = jnp.concatenate([table_z[0], table_z[1], table_z[0]], axis=0)
-    right = jnp.concatenate([table_z[0], table_z[0], table_z[1]], axis=0)
-    scaled = right[None] * jnp.tile(weights, (1, 3))[:, :, None]
-    circ = jnp.einsum("kw,ykz->ywz", left, scaled, preferred_element_type=F32)
+    left = wide(back_z)
+    right = jnp.concatenate([back_z[0], back_z[0], back_z[1]], axis=1)
+    scaled = right[None] * jnp.tile(weights, (1, 3))[:, None, :]
+    circ = jnp.einsum("wk,yzk->ywz", left, scaled, preferred_element_type=F32)
     high = lax.reduce_precision(circ, 8, 7)
-    return jnp.stack([high.astype(BF16), (circ - high).astype(BF16)])
+    return high.astype(BF16), (circ - high).astype(BF16)
 
 
 def conv_kernel(edge_ref, frame_ref, w1_ref, w2_ref, bias_ref, out_ref, cols_ref, acc_ref, *, nyb, hid):
@@ -352,25 +418,56 @@
     _, nc, zl, ny, nx = coil_sens.shape
     nz = measured.shape[2]
     yl = estimate.shape[2]
-    blocks = lax.axis_size(LINE)
+    slabs, cores = lax.axis_size("slab"), lax.axis_size("pencil")
     swap = [(0, 1), (1, 0)]
     at = lax.axis_index("coil")
-    table_y = jnp.asarray(split(line_dft(ny)))
-    table_z = jnp.asarray(split(line_dft(nz)))
-    table_x = jnp.asarray(split(line_dft(nx)))
-    back_y = jnp.asarray(split(line_dft(ny).T))
-
-    other = lax.ppermute(estimate.astype(HALF), "coil", swap).astype(F32)
-    framed = extended(estimate.astype(BF16), ((LINE, 1), ("coil", 2)), 2)
+    table_y = by_device(split(line_dft(ny)), slabs, cores)
+    back_y = wide(jnp.swapaxes(table_y, 1, 2))
+    table_y = wide(table_y)
+    back_z = by_device(split(line_dft(nz).T), slabs, cores)
+    table_x = split(line_dft(nx))
+
+    rounded = estimate.astype(BF16)
+    facing = jnp.where(at == 0, rounded[:, :, yl - 2 :], rounded[:, :, :2])
+    payload = jnp.concatenate([estimate.astype(HALF), facing.astype(HALF)], axis=2)
+    payload = lax.ppermute(payload, "coil", swap)
+    other = payload[:, :, :yl].astype(F32)
+    facing = payload[:, :, yl:].astype(BF16)
+    none = jnp.zeros_like(facing)
+    framed = jnp.concatenate(
+        [jnp.where(at == 0, none, facing), rounded, jnp.where(at == 0, facing, none)], axis=2
+    )
+
     place = jnp.reshape(at, (1,)).astype(jnp.int32)
-    sent = forward_y(place, estimate, other, coil_sens, table_y, blocks)
-    lines = lax.all_to_all(sent.astype(HALF), LINE, split_axis=0, concat_axis=0, tiled=True)
-    circ = circulants(sampling, table_z)
-    meas = measured_images(measured, sampling, table_z, table_x)
-    back = middle(lines.astype(F32), circ, meas)
+
+    def after(value, *others):
+        return lax.optimization_barrier((value,) + others)[0]
+
+    starts = [(first, nc // CHUNKS) for first in range(0, nc, nc // CHUNKS)]
+    lines, mine = [], estimate
+    for f, n in starts:
+        sent = forward_y(place, mine, other, coil_sens, table_y, slabs, f, n)
+        both, own = payloads(*sent, slabs)
+        mine = after(mine, both)
+        lines.append(delivered(both, own, slabs))
+    measured, sampling, framed, conv_in, conv_out = lax.optimization_barrier(
+        (measured, sampling, framed, conv_in, conv_out, mine)
+    )[:5]
+    framed = extended(framed, ((LINE, 1),), 2)
+    circ = circulants(sampling, back_z)
+    back_z = wide(back_z)
+    meas = {}
+    for f, n in starts:
+        meas[f] = measured_images(measured, sampling, table_x, back_z, f, n)
+    slices = []
+    for pieces, (f, n) in zip(lines, starts):
+        both = middle(pieces, circ, meas[f])
+        both, own = payloads(*both, slabs)
+        slices.append(delivered(both, own, slabs))
     regular = regularizer(framed, conv_in, bias_in, conv_out, nz)
-    slabs = lax.all_to_all(back.astype(HALF), LINE, split_axis=0, concat_axis=0, tiled=True)
-    partial = backward_y(slabs.astype(F32), coil_sens, back_y)
+    partial = jnp.zeros((2, zl, ny, nx), F32)
+    for pieces, (f, n) in zip(slices, starts):
+        partial = backward_y(pieces, coil_sens, back_y, partial, f)
     mine = lax.dynamic_slice_in_dim(partial, at * yl, yl, axis=2)
     theirs = lax.dynamic_slice_in_dim(partial, (1 - at) * yl, yl, axis=2)
     received = lax.ppermute((theirs * SCALE).astype(HALF), "coil", swap).astype(F32) * (1.0 / SCALE)
@@ -500,10 +597,19 @@
 def body(*arrays):
     estimate, coil_sens = arrays[0], arrays[1]
     _, zl, yl, nx = estimate.shape
-    ny = coil_sens.shape[3]
-    kyl = ny // lax.axis_size(LINE)
-    fits = zl % 16 == 0 and kyl % 16 == 0 and yl % 16 == 0 and nx == 128 and lax.axis_size("coil") == 2
-    return fast_body(*arrays) if fits else generic_body(*arrays)
+    nc, ny = coil_sens.shape[1], coil_sens.shape[3]
+    slabs = lax.axis_size("slab")
+    fits = (
+        nc % CHUNKS == 0
+        and nx == 128
+        and not (zl % 16 or yl % 16 or ny // lax.axis_size(LINE) % 16)
+        and slabs & (slabs - 1) == 0
+        and lax.axis_size("pencil") == 2
+        and lax.axis_size("coil") == 2
+    )
+    if not fits:
+        return generic_body(*arrays)
+    return fast_body(*arrays)
 
 
 def solution(mesh):

time: 319 us -> 323 us (1.013)
  the two profiles are of different devices: /device:TPU:15 before, /device:TPU:0 now
where the time goes in v2:
time: 323 us; the launch traced here: 322 us
  Pallas kernels  93.5 us (29%)
  waiting for transfers between devices  92.4 us (29%)
  other arithmetic  59.9 us (19%)
  starting transfers between devices  52 us (16%)
  matrix products  13.2 us (4%)
  local copies, waits for them, and re-layouts  9.41 us (3%)
    ppermute x12, waiting for transfers between devices, delivered(): moved[k] = lax.ppermute(payload, 'slab', [(i, i ^ k) for i in range(slabs)])  88.9 us
    ppermute x12, starting transfers between devices, delivered(): moved[k] = lax.ppermute(payload, 'slab', [(i, i ^ k) for i in range(slabs)])  42.6 us
    pallas_call x1, Pallas kernels, regularizer(): pl.pallas_call(functools.partial(conv_kernel, nyb=nyb, hid=hid), in_specs...  20.5 us
    pallas_call x2, Pallas kernels, backward_y(): pl.pallas_call(functools.partial(backward_y_kernel, len(pieces)), grid=(n...  19.6 us
    pallas_call x2, Pallas kernels, middle(): pl.pallas_call(functools.partial(middle_kernel, len(pieces)), grid=(kyl /...  19.4 us
    convert_element_type x12, other arithmetic, delivered(): moved[k] = moved[k].astype(F32)  18.9 us
    pallas_call x2, Pallas kernels, forward_y(): pl.pallas_call(forward_y_kernel, grid=(nc,), in_specs=[pl.BlockSpec(memor...  18 us
    pallas_call x2, Pallas kernels, measured_images(): pl.pallas_call(measured_kernel, grid=(kyl // kb,), in_specs=[block, block...  16 us
  transfers between devices with their start and end apart: 20, of which 7 were waited for; matrix products, arithmetic and copies ran while one was open for 19% of the time, Pallas kernels for 20%

profile of v2, /device:TPU:0, one launch (start us, length us, event | category | flops | bytes accessed | tf_op | source)
XLA Modules:
  0.0 321.7 jit_solution(12459753572325730648)
XLA Ops:
  0.0 1.4 convert_element_type.151
  2.4 3.0 collective-permute-start
  6.9 1.2 pad_maximum_fusion.18
  9.2 1.0 select_bitcast_fusion.2
  14.2 3.5 %collective-permute-done = f16[2,16,66,128]{3,1,2,0:T(8,128)(2,1)S(1)} collective-permute-done((f16[2,16,66,128]{3,1,2,0:T(8,128)(2,1)S(1)}, f16[2,16,66,128]{3,1,2,0:T(8,128)(2,1)S(1)}, u32[]{:S(2)}, u32[]{:S(2)}) %collective-permute-start) | collective-permute-done | bytes 540704 | tf_op jit(solution)/shard_map/ppermute | solution.py:433
  18.3 1.1 copy_convert_fusion.1.other_ref
  19.4 9.0 %shard_map.145 = (f32[4,2,2,256,128]{4,3,2,1,0:T(8,128)}, f32[4,2,2,256,128]{4,3,2,1,0:T(8,128)}) custom-call(s32[1]{0:T(128)} %bitcast.1.place_ref, f32[2,16,64,128]{3,2,1,0:T(8,128)} %own_ref.2, f32[2,16,64,128]{3,2,1,0:T(8,128)} %copy_convert_fusion.1.other_ref, bf16[2,4,16,128,128]{4,3,2,1,0:T(8,128)(2,1)} %refs_5_.3, ...), custom_call_target="tpu_custom_call" | custom-call | flops 1610612736 | bytes 7340032 | tf_op jit(solution)/shard_map/pallas_call | solution.py:127
  28.4 2.0 convert_element_type.154
  31.1 1.7 copy-done.7
  36.3 3.6 %fusion.4 = (bf16[2,16,2,128,128]{4,3,2,1,0:T(8,128)(2,1)}, bf16[2,16,2,128,128]{4,3,2,1,0:T(8,128)(2,1)}) fusion(bf16[2,128,2,128,1,1]{3,1,0,2,5,4:T(8,128)(2,1)S(1)} %copy-done.17, bf16[2,2,128,16,128,1]{4,3,2,1,0,5:T(8,128)(2,1)S(1)} %get-tuple-element.33, f32[2,128,16,2,128,1]{4,1,5,3,2,0:T(8,128)S(1)} %fusion.8), kind=kOutput, calls=%fused_computation.10 | convolution fusion | flops 542113792 | bytes 10616832 | tf_op jit(solution)/shard_map/pfqx,pczkf->ckqzx/dot_general | solution.py:260
  39.9 3.6 %fusion.3 = (bf16[2,16,2,128,128]{4,3,2,1,0:T(8,128)(2,1)}, bf16[2,16,2,128,128]{4,3,2,1,0:T(8,128)(2,1)}) fusion(bf16[2,128,2,128,1,1]{3,1,0,2,5,4:T(8,128)(2,1)S(1)} %copy-done.17, bf16[2,2,128,16,128,1]{4,3,2,1,0,5:T(8,128)(2,1)S(1)} %get-tuple-element.34, f32[2,128,16,2,128,1]{4,1,5,3,2,0:T(8,128)S(1)} %fusion.11), kind=kOutput, calls=%fused_computation.9 | convolution fusion | flops 542113792 | bytes 10616832 | tf_op jit(solution)/shard_map/pfqx,pczkf->ckqzx/dot_general | solution.py:260
  43.5 1.0 slice_convert_fusion.1
  44.5 0.9 pad_maximum_fusion.4
  45.5 1.0 pad_maximum_fusion.3
  47.4 9.0 %shard_map.146 = (f32[4,2,2,256,128]{4,3,2,1,0:T(8,128)}, f32[4,2,2,256,128]{4,3,2,1,0:T(8,128)}) custom-call(s32[1]{0:T(128)} %bitcast.1.place_ref, f32[2,16,64,128]{3,2,1,0:T(8,128)} %own_ref.2, f32[2,16,64,128]{3,2,1,0:T(8,128)} %copy_convert_fusion.1.other_ref, bf16[2,4,16,128,128]{4,3,2,1,0:T(8,128)(2,1)} %refs_5_.3, ...), custom_call_target="tpu_custom_call" | custom-call | flops 1610612736 | bytes 7340032 | tf_op jit(solution)/shard_map/pallas_call | solution.py:127
  56.3 1.8 convert_element_type.155
  58.5 2.7 collective-permute-start.18
  61.3 1.5 collective-permute-start.10
  62.7 2.6 collective-permute-start.11
  65.7 3.9 %fusion.2 = (bf16[16,256,256]{2,1,0:T(8,128)(2,1)}, bf16[16,256,256]{2,1,0:T(8,128)(2,1)}) fusion(bf16[256,256]{1,0:T(8,128)(2,1)S(1)} %bitcast.90, bf16[256,256]{1,0:T(8,128)(2,1)S(1)} %bitcast.88, bf16[16,768]{1,0:T(8,128)(2,1)S(1)} %bitcast.94, bf16[256,768]{1,0:T(8,128)(2,1)S(1)} %get-tuple-element.78), kind=kOutput, calls=%fused_computation.8 | convolution fusion | flops 1619132416 | bytes 4874240 | tf_op jit(solution)/shard_map/wk,yzk->ywz/dot_general | solution.py:284
  69.5 8.0 %shard_map.149.refs_7_ = f32[16,256,256]{2,1,0:T(8,128)} custom-call(bf16[2,16,256,128]{3,2,1,0:T(8,128)(2,1)} %bitcast.81, bf16[2,16,256,128]{3,2,1,0:T(8,128)(2,1)} %bitcast.80, bf16[256,768]{1,0:T(8,128)(2,1)} %get-tuple-element.77.table_ref), custom_call_target="tpu_custom_call" | custom-call | flops 1610612736 | bytes 8388608 | tf_op jit(solution)/shard_map/pallas_call | solution.py:266
  78.0 8.8 %collective-permute-done.10 = f16[2,2,2,256,128]{4,3,2,1,0:T(8,128)(2,1)} collective-permute-done((f16[2,2,2,256,128]{4,3,2,1,0:T(8,128)(2,1)}, f16[2,2,2,256,128]{4,3,2,1,0:T(8,128)(2,1)}, u32[]{:S(2)}, u32[]{:S(2)}) %collective-permute-start.10) | collective-permute-done | bytes 524320 | tf_op jit(solution)/shard_map/ppermute | solution.py:70
  86.8 2.1 convert_element_type.171.refs_2_
  88.9 12.1 %collective-permute-done.11 = f16[2,2,2,256,128]{4,3,2,1,0:T(8,128)(2,1)} collective-permute-done((f16[2,2,2,256,128]{4,3,2,1,0:T(8,128)(2,1)}, f16[2,2,2,256,128]{4,3,2,1,0:T(8,128)(2,1)}, u32[]{:S(2)}, u32[]{:S(2)}) %collective-permute-start.11) | collective-permute-done | bytes 524320 | tf_op jit(solution)/shard_map/ppermute | solution.py:70
  101.0 2.1 convert_element_type.172.refs_3_
  103.1 2.1 convert_element_type.173.refs_4_
  105.2 9.7 %shard_map.150 = (f32[4,2,2,256,128]{4,3,2,1,0:T(8,128)}, f32[4,2,2,256,128]{4,3,2,1,0:T(8,128)}) custom-call(f32[4,2,2,256,128]{4,3,2,1,0:T(8,128)} %get-tuple-element.19.refs_0_, f32[1,2,2,256,128]{4,3,2,1,0:T(8,128)} %get-tuple-element.48.refs_1_, f32[2,2,2,256,128]{4,3,2,1,0:T(8,128)} %convert_element_type.171.refs_2_, ...), custom_call_target="tpu_custom_call" | custom-call | flops 1610612736 | bytes 12582912 | tf_op jit(solution)/shard_map/pallas_call | solution.py:177
  115.0 2.8 convert_element_type.176
  118.1 2.2 fusion.31
  121.2 2.5 collective-permute-start.5
  124.7 8.5 %collective-permute-start.4 = (f16[2,2,2,256,128]{4,3,2,1,0:T(8,128)(2,1)}, f16[2,2,2,256,128]{4,3,2,1,0:T(8,128)(2,1)}, u32[]{:S(2)}, u32[]{:S(2)}) collective-permute-start(f16[2,2,2,256,128]{4,3,2,1,0:T(8,128)(2,1)} %pad_maximum_fusion.6), channel_id=1, source_target_pairs={{0,8},{4,12},{8,0},{12,4},{1,9},{5,13},{9,1},{13,5},{2,10},{6,14},... | collective-permute-start | bytes 1572872 | tf_op jit(solution)/shard_map/ppermute | solution.py:70
  134.5 8.0 %shard_map.147.refs_7_ = f32[16,256,256]{2,1,0:T(8,128)} custom-call(bf16[2,16,256,128]{3,2,1,0:T(8,128)(2,1)} %bitcast.79, bf16[2,16,256,128]{3,2,1,0:T(8,128)(2,1)} %bitcast.78, bf16[256,768]{1,0:T(8,128)(2,1)} %get-tuple-element.77.table_ref), custom_call_target="tpu_custom_call" | custom-call | flops 1610612736 | bytes 8388608 | tf_op jit(solution)/shard_map/pallas_call | solution.py:266
  142.9 1.3 collective-permute-start.19
  144.2 2.1 convert_element_type.159.refs_4_
  146.3 24.9 %collective-permute-done.4 = f16[2,2,2,256,128]{4,3,2,1,0:T(8,128)(2,1)} collective-permute-done((f16[2,2,2,256,128]{4,3,2,1,0:T(8,128)(2,1)}, f16[2,2,2,256,128]{4,3,2,1,0:T(8,128)(2,1)}, u32[]{:S(2)}, u32[]{:S(2)}) %collective-permute-start.4) | collective-permute-done | bytes 524320 | tf_op jit(solution)/shard_map/ppermute | solution.py:70
  171.2 2.1 convert_element_type.158.refs_3_
  173.3 2.1 convert_element_type.157.refs_2_
  175.4 9.7 %shard_map.148 = (f32[4,2,2,256,128]{4,3,2,1,0:T(8,128)}, f32[4,2,2,256,128]{4,3,2,1,0:T(8,128)}) custom-call(f32[4,2,2,256,128]{4,3,2,1,0:T(8,128)} %get-tuple-element.22.refs_0_, f32[1,2,2,256,128]{4,3,2,1,0:T(8,128)} %get-tuple-element.65.refs_1_, f32[2,2,2,256,128]{4,3,2,1,0:T(8,128)} %convert_element_type.157.refs_2_, ...), custom_call_target="tpu_custom_call" | custom-call | flops 1610612736 | bytes 12582912 | tf_op jit(solution)/shard_map/pallas_call | solution.py:177
  185.1 2.0 convert_element_type.165
  187.8 2.2 fusion.27
  190.1 2.5 collective-permute-start.16
  193.0 2.0 collective-permute-start.14
  195.0 1.0 fusion.29
  196.5 2.5 collective-permute-start.9
  198.9 7.9 %collective-permute-done.16 = f16[2,2,2,256,128]{4,3,2,1,0:T(8,128)(2,1)S(1)} collective-permute-done((f16[2,2,2,256,128]{4,3,2,1,0:T(8,128)(2,1)S(1)}, f16[2,2,2,256,128]{4,3,2,1,0:T(8,128)(2,1)S(1)}, u32[]{:S(2)}, u32[]{:S(2)}) %collective-permute-start.16) | collective-permute-done | bytes 524320 | tf_op jit(solution)/shard_map/ppermute | solution.py:70
  206.9 20.1 %collective-permute-start.7 = (f16[2,2,2,256,128]{4,3,2,1,0:T(8,128)(2,1)S(1)}, f16[2,2,2,256,128]{4,3,2,1,0:T(8,128)(2,1)S(1)}, u32[]{:S(2)}, u32[]{:S(2)}) collective-permute-start(f16[2,2,2,256,128]{4,3,2,1,0:T(8,128)(2,1)S(1)} %pad_maximum_fusion.8), channel_id=1, source_target_pairs={{0,4},{4,0},{8,12},{12,8},{1,5},{5,1},{9,13},{13,9},{2,6},{6,2},{1... | collective-permute-start | bytes 1572872 | tf_op jit(solution)/shard_map/ppermute | solution.py:70
  227.0 1.0 multiply_reduce_fusion.1
  228.0 1.2 multiply_reduce_fusion
  229.2 2.2 fusion.18.frame_ref
  231.4 1.0 convert_element_type.180.refs_4_
  232.4 27.8 %collective-permute-done.15 = f16[2,2,2,256,128]{4,3,2,1,0:T(8,128)(2,1)S(1)} collective-permute-done((f16[2,2,2,256,128]{4,3,2,1,0:T(8,128)(2,1)S(1)}, f16[2,2,2,256,128]{4,3,2,1,0:T(8,128)(2,1)S(1)}, u32[]{:S(2)}, u32[]{:S(2)}) %collective-permute-start.15) | collective-permute-done | bytes 524320 | tf_op jit(solution)/shard_map/ppermute | solution.py:70
  260.2 1.1 convert_element_type.179.refs_3_
  261.2 1.0 convert_element_type.178.refs_2_
  262.3 1.6 broadcast_in_dim.41.refs_7_
  263.9 9.8 %shard_map.151.refs_7_ = f32[2,16,128,128]{3,2,1,0:T(8,128)} custom-call(f32[4,2,2,256,128]{4,3,2,1,0:T(8,128)} %get-tuple-element.28.refs_0_, f32[1,2,2,256,128]{4,3,2,1,0:T(8,128)} %get-tuple-element.47.refs_1_, f32[2,2,2,256,128]{4,3,2,1,0:T(8,128)} %convert_element_type.178.refs_2_, ...), custom_call_target="tpu_custom_call", output_to_operand_aliasing={{}: (7, {})} | custom-call | flops 1610612736 | bytes 7340032 | tf_op jit(solution)/shard_map/pallas_call | solution.py:227
  273.7 1.0 convert_element_type.169.refs_4_
  274.7 7.4 %collective-permute-done.8 = f16[2,2,2,256,128]{4,3,2,1,0:T(8,128)(2,1)S(1)} collective-permute-done((f16[2,2,2,256,128]{4,3,2,1,0:T(8,128)(2,1)S(1)}, f16[2,2,2,256,128]{4,3,2,1,0:T(8,128)(2,1)S(1)}, u32[]{:S(2)}, u32[]{:S(2)}) %collective-permute-start.8) | collective-permute-done | bytes 524320 | tf_op jit(solution)/shard_map/ppermute | solution.py:70
  282.1 1.1 convert_element_type.168.refs_3_
  283.2 1.0 convert_element_type.167.refs_2_
  284.2 9.8 %shard_map.152 = f32[2,16,128,128]{3,2,1,0:T(8,128)} custom-call(f32[4,2,2,256,128]{4,3,2,1,0:T(8,128)} %get-tuple-element.26.refs_0_, f32[1,2,2,256,128]{4,3,2,1,0:T(8,128)} %get-tuple-element.58.refs_1_, f32[2,2,2,256,128]{4,3,2,1,0:T(8,128)} %convert_element_type.167.refs_2_, ...), custom_call_target="tpu_custom_call", output_to_operand_aliasing={{}: (7, {})} | custom-call | flops 1610612736 | bytes 7340032 | tf_op jit(solution)/shard_map/pallas_call | solution.py:227
  294.0 2.2 multiply_convert_fusion
  296.2 1.5 collective-permute-start.17
  298.6 20.5 %regularizer.1 = f32[2,16,64,128]{3,2,1,0:T(8,128)} custom-call(s32[4]{0:T(128)} %pad_add_fusion.edge_ref, f32[2,20,72,128]{3,2,1,0:T(8,128)} %fusion.18.frame_ref, bf16[576,432]{1,0:T(8,128)(2,1)} %bitcast.84, bf16[288,576]{1,0:T(8,128)(2,1)} %bitcast.91, f32[576,128]{1,0:T(8,128)} %broadcast_in_dim.43.bias_ref), custom_call_target="tpu_custom_call" | custom-call | flops 7644119040 | bytes 4194304 | tf_op jit(solution)/shard_map/regularizer/pallas_call | solution.py:388
  319.0 2.7 subtract_subtract_fusion
  (133 shorter events, 20.0 us)
Async XLA Ops:
  0.0 1.5 copy-start.1
  0.0 5.4 %copy-start.10 = (bf16[4,4,2,16,256]{4,3,2,1,0:T(8,128)(2,1)S(1)}, bf16[4,4,2,16,256]{4,3,2,1,0:T(8,128)(2,1)}, u32[]{:S(2)}) copy-start(bf16[4,4,2,16,256]{4,3,2,1,0:T(8,128)(2,1)} %constant.66) | copy-start | bytes 786436
  0.0 5.4 %copy-start.11 = (bf16[4,4,2,16,256]{4,3,2,1,0:T(8,128)(2,1)S(1)}, bf16[4,4,2,16,256]{4,3,2,1,0:T(8,128)(2,1)}, u32[]{:S(2)}) copy-start(bf16[4,4,2,16,256]{4,3,2,1,0:T(8,128)(2,1)} %constant.71) | copy-start | bytes 786436
  1.5 4.7 %copy-start.12 = (bf16[4,4,2,16,256]{4,3,2,1,0:T(8,128)(2,1)S(1)}, bf16[4,4,2,16,256]{4,3,2,1,0:T(8,128)(2,1)}, u32[]{:S(2)}) copy-start(bf16[4,4,2,16,256]{4,3,2,1,0:T(8,128)(2,1)} %constant.60) | copy-start | bytes 786436
  1.5 4.7 %copy-start.13 = (bf16[4,4,2,16,256]{4,3,2,1,0:T(8,128)(2,1)S(1)}, bf16[4,4,2,16,256]{4,3,2,1,0:T(8,128)(2,1)}, u32[]{:S(2)}) copy-start(bf16[4,4,2,16,256]{4,3,2,1,0:T(8,128)(2,1)} %constant.65) | copy-start | bytes 786436
  2.4 15.3 %collective-permute-start = (f16[2,16,66,128]{3,1,2,0:T(8,128)(2,1)S(1)}, f16[2,16,66,128]{3,1,2,0:T(8,128)(2,1)S(1)}, u32[]{:S(2)}, u32[]{:S(2)}) collective-permute-start(f16[2,16,66,128]{3,1,2,0:T(8,128)(2,1)S(1)} %pad_maximum_fusion.1), channel_id=1, source_target_pairs={{0,2},{2,0},{1,3},{3,1},{4,6},{6,4},{5,7},{7,5},{8,10},{10,8},{9,1... | collective-permute-start | bytes 1622024 | tf_op jit(solution)/shard_map/ppermute | solution.py:433
  8.9 1.4 copy-start.15
  8.9 1.4 copy-start.16
  9.0 2.9 copy-start.25
  10.4 7.7 %copy-start.21 = (s32[128,16]{0,1:T(8,128)S(1)}, s32[128,16]{0,1:T(8,128)}, u32[]{:S(2)}) copy-start(s32[128,16]{0,1:T(8,128)} %param.18) | copy-start | bytes 24580
  18.0 17.6 %copy-start.8 = (bf16[2,16,68,128]{3,2,1,0:T(8,128)(2,1)}, bf16[2,16,68,128]{3,2,1,0:T(8,128)(2,1)S(1)}, u32[]{:S(2)}) copy-start(bf16[2,16,68,128]{3,2,1,0:T(8,128)(2,1)S(1)} %pad_maximum_fusion) | copy-start | bytes 1671172
  28.4 2.2 copy-start.6
  30.4 13.1 %collective-permute-start.1 = (f16[4,2,2,256,128]{4,3,2,1,0:T(8,128)(2,1)S(1)}, f16[4,2,2,256,128]{4,3,2,1,0:T(8,128)(2,1)S(1)}, u32[]{:S(2)}, u32[]{:S(2)}) collective-permute-start(f16[4,2,2,256,128]{4,3,2,1,0:T(8,128)(2,1)S(1)} %convert_element_type.154), channel_id=1, source_target_pairs={{0,1},{1,0},{2,3},{3,2},{4,5},{5,4},{6,7},{7,6},{8,9},{9,8},{10,11... | collective-permute-start | bytes 3145736 | tf_op jit(solution)/shard_map/ppermute | solution.py:62
  30.6 2.2 copy-start.7
  32.8 0.9 copy-start.14
  34.7 1.7 copy-start.17
  58.1 60.0 %collective-permute-start.2 = (f16[4,2,2,256,128]{4,3,2,1,0:T(8,128)(2,1)S(1)}, f16[4,2,2,256,128]{4,3,2,1,0:T(8,128)(2,1)}, u32[]{:S(2)}, u32[]{:S(2)}) collective-permute-start(f16[4,2,2,256,128]{4,3,2,1,0:T(8,128)(2,1)S(1)} %convert_element_type.155), channel_id=1, source_target_pairs={{0,1},{1,0},{2,3},{3,2},{4,5},{5,4},{6,7},{7,6},{8,9},{9,8},{10,11... | collective-permute-start | bytes 3145736 | tf_op jit(solution)/shard_map/ppermute | solution.py:62
  58.5 137.9 %collective-permute-start.18 = (bf16[2,2,68,128]{3,2,1,0:T(8,128)(2,1)}, bf16[2,2,68,128]{3,2,1,0:T(8,128)(2,1)}, u32[]{:S(2)}, u32[]{:S(2)}) collective-permute-start(bf16[2,2,68,128]{3,2,1,0:T(8,128)(2,1)} %get-tuple-element.69), channel_id=1, source_target_pairs={{0,1},{1,4},{4,5},{5,8},{8,9},{9,12},{12,13},{2,3},{3,6},{6,7},{7,... | collective-permute-start | bytes 208904 | tf_op jit(solution)/shard_map/ppermute | solution.py:411
  61.3 25.5 %collective-permute-start.10 = (f16[2,2,2,256,128]{4,3,2,1,0:T(8,128)(2,1)}, f16[2,2,2,256,128]{4,3,2,1,0:T(8,128)(2,1)}, u32[]{:S(2)}, u32[]{:S(2)}) collective-permute-start(f16[2,2,2,256,128]{4,3,2,1,0:T(8,128)(2,1)} %pad_maximum_fusion.4), channel_id=1, source_target_pairs={{0,4},{4,0},{8,12},{12,8},{1,5},{5,1},{9,13},{13,9},{2,6},{6,2},{1... | collective-permute-start | bytes 1572872 | tf_op jit(solution)/shard_map/ppermute | solution.py:70
  62.7 38.3 %collective-permute-start.11 = (f16[2,2,2,256,128]{4,3,2,1,0:T(8,128)(2,1)}, f16[2,2,2,256,128]{4,3,2,1,0:T(8,128)(2,1)}, u32[]{:S(2)}, u32[]{:S(2)}) collective-permute-start(f16[2,2,2,256,128]{4,3,2,1,0:T(8,128)(2,1)} %pad_maximum_fusion.3), channel_id=1, source_target_pairs={{0,8},{4,12},{8,0},{12,4},{1,9},{5,13},{9,1},{13,5},{2,10},{6,14},... | collective-permute-start | bytes 1572872 | tf_op jit(solution)/shard_map/ppermute | solution.py:70
  65.3 37.8 %collective-permute-start.12 = (f16[2,2,2,256,128]{4,3,2,1,0:T(8,128)(2,1)}, f16[2,2,2,256,128]{4,3,2,1,0:T(8,128)(2,1)}, u32[]{:S(2)}, u32[]{:S(2)}) collective-permute-start(f16[2,2,2,256,128]{4,3,2,1,0:T(8,128)(2,1)} %pad_maximum_fusion.2), channel_id=1, source_target_pairs={{0,12},{4,8},{8,4},{12,0},{1,13},{5,9},{9,5},{13,1},{2,14},{6,10},... | collective-permute-start | bytes 1572872 | tf_op jit(solution)/shard_map/ppermute | solution.py:70
  65.7 3.9 %copy-start.24 = (bf16[32,2,3,3,3]{0,1,4,3,2:T(2,128)(2,1)S(1)}, bf16[32,2,3,3,3]{0,1,4,3,2:T(2,128)(2,1)}, u32[]{:S(2)}) copy-start(bf16[32,2,3,3,3]{0,1,4,3,2:T(2,128)(2,1)} %param.20) | copy-start | bytes 10372
  69.5 8.0 %copy-start.4 = (f32[4,2,2,256,128]{4,3,2,1,0:T(8,128)S(1)}, f32[4,2,2,256,128]{4,3,2,1,0:T(8,128)}, u32[]{:S(2)}) copy-start(f32[4,2,2,256,128]{4,3,2,1,0:T(8,128)} %get-tuple-element.22.refs_0_) | copy-start | bytes 6291460
  117.8 70.0 %collective-permute-start.13 = (f16[4,2,2,256,128]{4,3,2,1,0:T(8,128)(2,1)}, f16[4,2,2,256,128]{4,3,2,1,0:T(8,128)(2,1)}, u32[]{:S(2)}, u32[]{:S(2)}) collective-permute-start(f16[4,2,2,256,128]{4,3,2,1,0:T(8,128)(2,1)} %convert_element_type.176), channel_id=1, source_target_pairs={{0,1},{1,0},{2,3},{3,2},{4,5},{5,4},{6,7},{7,6},{8,9},{9,8},{10,11... | collective-permute-start | bytes 3145736 | tf_op jit(solution)/shard_map/ppermute | solution.py:62
  120.3 13.9 %copy-start.22 = (bf16[18,432,1]{1,0,2:T(8,128)(2,1)S(1)}, bf16[18,432,1]{1,0,2:T(8,128)(2,1)}, u32[]{:S(2)}) copy-start(bf16[18,432,1]{1,0,2:T(8,128)(2,1)} %constant.81) | copy-start | bytes 46660
  120.3 14.1 %copy-start.23 = (bf16[2,32,3,3,3]{1,0,4,3,2:T(2,128)(2,1)S(1)}, bf16[2,32,3,3,3]{1,0,4,3,2:T(2,128)(2,1)}, u32[]{:S(2)}) copy-start(bf16[2,32,3,3,3]{1,0,4,3,2:T(2,128)(2,1)} %param.22) | copy-start | bytes 10372
  121.2 21.6 %collective-permute-start.5 = (f16[2,2,2,256,128]{4,3,2,1,0:T(8,128)(2,1)}, f16[2,2,2,256,128]{4,3,2,1,0:T(8,128)(2,1)}, u32[]{:S(2)}, u32[]{:S(2)}) collective-permute-start(f16[2,2,2,256,128]{4,3,2,1,0:T(8,128)(2,1)} %pad_maximum_fusion.7), channel_id=1, source_target_pairs={{0,12},{4,8},{8,4},{12,0},{1,13},{5,9},{9,5},{13,1},{2,14},{6,10},... | collective-permute-start | bytes 1572872 | tf_op jit(solution)/shard_map/ppermute | solution.py:70
  124.7 46.5 %collective-permute-start.4 = (f16[2,2,2,256,128]{4,3,2,1,0:T(8,128)(2,1)}, f16[2,2,2,256,128]{4,3,2,1,0:T(8,128)(2,1)}, u32[]{:S(2)}, u32[]{:S(2)}) collective-permute-start(f16[2,2,2,256,128]{4,3,2,1,0:T(8,128)(2,1)} %pad_maximum_fusion.6), channel_id=1, source_target_pairs={{0,8},{4,12},{8,0},{12,4},{1,9},{5,13},{9,1},{13,5},{2,10},{6,14},... | collective-permute-start | bytes 1572872 | tf_op jit(solution)/shard_map/ppermute | solution.py:70
  134.1 39.2 %collective-permute-start.3 = (f16[2,2,2,256,128]{4,3,2,1,0:T(8,128)(2,1)}, f16[2,2,2,256,128]{4,3,2,1,0:T(8,128)(2,1)}, u32[]{:S(2)}, u32[]{:S(2)}) collective-permute-start(f16[2,2,2,256,128]{4,3,2,1,0:T(8,128)(2,1)} %pad_maximum_fusion.5), channel_id=1, source_target_pairs={{0,4},{4,0},{8,12},{12,8},{1,5},{5,1},{9,13},{13,9},{2,6},{6,2},{1... | collective-permute-start | bytes 1572872 | tf_op jit(solution)/shard_map/ppermute | solution.py:70
  134.4 8.0 %copy-start.20 = (bf16[32,576,1]{1,0,2:T(8,128)(2,1)S(1)}, bf16[32,576,1]{1,0,2:T(8,128)(2,1)}, u32[]{:S(2)}) copy-start(bf16[32,576,1]{1,0,2:T(8,128)(2,1)} %constant.82) | copy-start | bytes 110596
  134.4 8.2 %copy-start.3 = (f32[4,2,2,256,128]{4,3,2,1,0:T(8,128)S(1)}, f32[4,2,2,256,128]{4,3,2,1,0:T(8,128)}, u32[]{:S(2)}) copy-start(f32[4,2,2,256,128]{4,3,2,1,0:T(8,128)} %get-tuple-element.28.refs_0_) | copy-start | bytes 6291460
  142.9 56.1 %collective-permute-start.19 = (bf16[2,2,68,128]{3,2,1,0:T(8,128)(2,1)}, bf16[2,2,68,128]{3,2,1,0:T(8,128)(2,1)}, u32[]{:S(2)}, u32[]{:S(2)}) collective-permute-start(bf16[2,2,68,128]{3,2,1,0:T(8,128)(2,1)} %get-tuple-element.70), channel_id=1, source_target_pairs={{1,0},{4,1},{5,4},{8,5},{9,8},{12,9},{13,12},{3,2},{6,3},{7,6},{10... | collective-permute-start | bytes 208904 | tf_op jit(solution)/shard_map/ppermute | solution.py:412
  185.1 2.2 copy-start.5
  187.0 5.9 %collective-permute-start.6 = (f16[4,2,2,256,128]{4,3,2,1,0:T(8,128)(2,1)S(1)}, f16[4,2,2,256,128]{4,3,2,1,0:T(8,128)(2,1)S(1)}, u32[]{:S(2)}, u32[]{:S(2)}) collective-permute-start(f16[4,2,2,256,128]{4,3,2,1,0:T(8,128)(2,1)S(1)} %convert_element_type.165), channel_id=1, source_target_pairs={{0,1},{1,0},{2,3},{3,2},{4,5},{5,4},{6,7},{7,6},{8,9},{9,8},{10,11... | collective-permute-start | bytes 3145736 | tf_op jit(solution)/shard_map/ppermute | solution.py:62
  190.1 16.8 %collective-permute-start.16 = (f16[2,2,2,256,128]{4,3,2,1,0:T(8,128)(2,1)S(1)}, f16[2,2,2,256,128]{4,3,2,1,0:T(8,128)(2,1)S(1)}, u32[]{:S(2)}, u32[]{:S(2)}) collective-permute-start(f16[2,2,2,256,128]{4,3,2,1,0:T(8,128)(2,1)S(1)} %pad_maximum_fusion.13), channel_id=1, source_target_pairs={{0,12},{4,8},{8,4},{12,0},{1,13},{5,9},{9,5},{13,1},{2,14},{6,10},... | collective-permute-start | bytes 1572872 | tf_op jit(solution)/shard_map/ppermute | solution.py:70
  192.7 67.5 %collective-permute-start.15 = (f16[2,2,2,256,128]{4,3,2,1,0:T(8,128)(2,1)S(1)}, f16[2,2,2,256,128]{4,3,2,1,0:T(8,128)(2,1)S(1)}, u32[]{:S(2)}, u32[]{:S(2)}) collective-permute-start(f16[2,2,2,256,128]{4,3,2,1,0:T(8,128)(2,1)S(1)} %pad_maximum_fusion.12), channel_id=1, source_target_pairs={{0,8},{4,12},{8,0},{12,4},{1,9},{5,13},{9,1},{13,5},{2,10},{6,14},... | collective-permute-start | bytes 1572872 | tf_op jit(solution)/shard_map/ppermute | solution.py:70
  193.0 68.3 %collective-permute-start.14 = (f16[2,2,2,256,128]{4,3,2,1,0:T(8,128)(2,1)S(1)}, f16[2,2,2,256,128]{4,3,2,1,0:T(8,128)(2,1)S(1)}, u32[]{:S(2)}, u32[]{:S(2)}) collective-permute-start(f16[2,2,2,256,128]{4,3,2,1,0:T(8,128)(2,1)S(1)} %pad_maximum_fusion.11), channel_id=1, source_target_pairs={{0,4},{4,0},{8,12},{12,8},{1,5},{5,1},{9,13},{13,9},{2,6},{6,2},{1... | collective-permute-start | bytes 1572872 | tf_op jit(solution)/shard_map/ppermute | solution.py:70
  196.0 31.0 %copy-start.19 = (f32[3,16,576]{2,1,0:T(8,128)S(1)}, f32[3,16,576]{2,1,0:T(8,128)}, u32[]{:S(2)}) copy-start(f32[3,16,576]{2,1,0:T(8,128)} %constant.78) | copy-start | bytes 331780
  196.0 32.0 %copy-start.18 = (f32[3,18,432]{2,1,0:T(8,128)S(1)}, f32[3,18,432]{2,1,0:T(8,128)}, u32[]{:S(2)}) copy-start(f32[3,18,432]{2,1,0:T(8,128)} %constant.77) | copy-start | bytes 279940
  196.1 33.1 %copy-start.9 = (bf16[2,16,68,128]{3,2,1,0:T(8,128)(2,1)S(1)}, bf16[2,16,68,128]{3,2,1,0:T(8,128)(2,1)}, u32[]{:S(2)}) copy-start(bf16[2,16,68,128]{3,2,1,0:T(8,128)(2,1)} %copy-done.8) | copy-start | bytes 1671172
  196.5 77.3 %collective-permute-start.9 = (f16[2,2,2,256,128]{4,3,2,1,0:T(8,128)(2,1)S(1)}, f16[2,2,2,256,128]{4,3,2,1,0:T(8,128)(2,1)S(1)}, u32[]{:S(2)}, u32[]{:S(2)}) collective-permute-start(f16[2,2,2,256,128]{4,3,2,1,0:T(8,128)(2,1)S(1)} %pad_maximum_fusion.10), channel_id=1, source_target_pairs={{0,12},{4,8},{8,4},{12,0},{1,13},{5,9},{9,5},{13,1},{2,14},{6,10},... | collective-permute-start | bytes 1572872 | tf_op jit(solution)/shard_map/ppermute | solution.py:70
  198.9 83.2 %collective-permute-start.8 = (f16[2,2,2,256,128]{4,3,2,1,0:T(8,128)(2,1)S(1)}, f16[2,2,2,256,128]{4,3,2,1,0:T(8,128)(2,1)S(1)}, u32[]{:S(2)}, u32[]{:S(2)}) collective-permute-start(f16[2,2,2,256,128]{4,3,2,1,0:T(8,128)(2,1)S(1)} %pad_maximum_fusion.9), channel_id=1, source_target_pairs={{0,8},{4,12},{8,0},{12,4},{1,9},{5,13},{9,1},{13,5},{2,10},{6,14},... | collective-permute-start | bytes 1572872 | tf_op jit(solution)/shard_map/ppermute | solution.py:70
  206.9 76.3 %collective-permute-start.7 = (f16[2,2,2,256,128]{4,3,2,1,0:T(8,128)(2,1)S(1)}, f16[2,2,2,256,128]{4,3,2,1,0:T(8,128)(2,1)S(1)}, u32[]{:S(2)}, u32[]{:S(2)}) collective-permute-start(f16[2,2,2,256,128]{4,3,2,1,0:T(8,128)(2,1)S(1)} %pad_maximum_fusion.8), channel_id=1, source_target_pairs={{0,4},{4,0},{8,12},{12,8},{1,5},{5,1},{9,13},{13,9},{2,6},{6,2},{1... | collective-permute-start | bytes 1572872 | tf_op jit(solution)/shard_map/ppermute | solution.py:70
  296.2 22.8 %collective-permute-start.17 = (f16[2,16,64,128]{3,2,1,0:T(8,128)(2,1)}, f16[2,16,64,128]{3,2,1,0:T(8,128)(2,1)}, u32[]{:S(2)}, u32[]{:S(2)}) collective-permute-start(f16[2,16,64,128]{3,2,1,0:T(8,128)(2,1)} %multiply_convert_fusion), channel_id=1, source_target_pairs={{0,2},{2,0},{1,3},{3,1},{4,6},{6,4},{5,7},{7,5},{8,10},{10,8},{9,1... | collective-permute-start | bytes 1572872 | tf_op jit(solution)/shard_map/ppermute | solution.py:473
  298.5 20.5 %copy-start = (f32[2,16,128,128]{3,2,1,0:T(8,128)S(1)}, f32[2,16,128,128]{3,2,1,0:T(8,128)}, u32[]{:S(2)}) copy-start(f32[2,16,128,128]{3,2,1,0:T(8,128)} %shard_map.152) | copy-start | bytes 6291460
  298.5 20.5 %copy-start.2 = (f32[2,16,64,128]{3,2,1,0:T(8,128)S(1)}, f32[2,16,64,128]{3,2,1,0:T(8,128)}, u32[]{:S(2)}) copy-start(f32[2,16,64,128]{3,2,1,0:T(8,128)} %own_ref.2) | copy-start | bytes 3145732
